TPU v7x, 512 devices: a whole 4x4x16 slice. The times are simulated.
512 devices in a mesh: seq: 32 (over x, z_lo, core), exp: 16 (over z_hi, y).
Axes of the slice: x: 4, y: 4, z: 16 (z_hi: 4, z_lo: 4; z = z_hi * 4 + z_lo), core: 2. Of those that a mesh axis runs over, the one named last changes fastest.
Arguments:
- tokens: bfloat16 [2, 16384, 1024], P(None, 'seq'), may hold values from -48 to 48
- router: bfloat16 [1024, 2048], P(None, 'exp'), may hold values from -4 to 4
- w_in: bfloat16 [512, 1024, 512], P(('exp', 'seq')), may hold values from -0.1875 to 0.1875
- w_out: bfloat16 [512, 512, 1024], P(('exp', 'seq')), may hold values from -0.125 to 0.125
Outputs:
- mixed: bfloat16 [2, 16384, 1024], P(None, ('seq', 'exp'))
All inputs are finite; a program needn't handle non-finite values.
Results may differ from a plain program's by a relative error of at most 0.015.
Values may be sent and summed in bfloat16 or wider, within the bound.
No kernel may reach another device: no remote copies, remote signals or barrier semaphores. Data moves between devices by JAX's collectives and lax.ppermute only.
A program may use at most 64 MiB of HBM per device.

v0:
```python
import jax
import jax.numpy as jnp
from jax import lax
from jax.sharding import Mesh
from jax.sharding import PartitionSpec as P

SLOTS = 16
SEQ = ("seq_0", "seq_1", "seq_2")
EXP = ("exp_0", "exp_1")
EXP_SEQ = ("exp_0", "exp_1", "seq_0", "seq_1", "seq_2")
SEQ_EXP = ("seq_0", "seq_1", "seq_2", "exp_0", "exp_1")


def copy_for_each(shard, axis):
    copies = jnp.broadcast_to(shard, (lax.axis_size(axis), *shard.shape))
    return lax.all_to_all(copies, axis, split_axis=0, concat_axis=0, tiled=True)


def all_in_one(shard, axis):
    leaves = jax.tree.leaves(shard)
    order = sorted(range(len(leaves)), key=lambda k: -leaves[k].size)
    width = (1, *leaves[order[0]].shape)[-1]
    lines = [
        jnp.pad(leaves[k].reshape(-1), (0, -leaves[k].size % width)).reshape(-1, width)
        for k in order
    ]
    both, at, found = (copy_for_each(jnp.concatenate(lines), axis), 0, {})
    for k, line in zip(order, lines):
        share = both[:, at : at + len(line)].reshape(len(both), -1)
        found[k] = share[:, : leaves[k].size].reshape(-1, *leaves[k].shape)
        at += len(line)
    numbers = iter(range(len(leaves)))
    return jax.tree.map(lambda _: found[next(numbers)], shard)


def folded_in_pairs(pieces, combine):
    while len(jax.tree.leaves(pieces)[0]) > 1:
        pieces = jax.vmap(combine)(
            *(jax.tree.map(lambda part: part[side::2], pieces) for side in (0, 1))
        )
    return jax.tree.map(lambda part: part[0], pieces)


def merged(shard, axis, combine):
    pieces = all_in_one(shard, axis)
    return folded_in_pairs(pieces, combine)


def rows_for(lines, devices):
    spare = -lines.shape[0] % devices
    if not spare:
        return lines
    return jnp.concatenate([lines, jnp.zeros((spare, *lines.shape[1:]), lines.dtype)])


def in_order(tiles, dim):
    tiles = jnp.moveaxis(tiles, 0, dim)
    lengths = tiles.shape
    return tiles.reshape(*lengths[:dim], lengths[dim] * lengths[dim + 1], *lengths[dim + 2 :])


def gathered_by_axis(shard, axes, dim):
    far, near = axes
    tiles = copy_for_each(copy_for_each(shard, far), near)
    return in_order(tiles.swapaxes(0, 1).reshape(-1, *shard.shape), dim)


def split_up(shard, dim, devices):
    before, after = (shard.shape[:dim], shard.shape[dim + 1 :])
    return jnp.moveaxis(shard.reshape(*before, devices, -1, *after), dim, 0)


def sent_and_summed(shard, axis, dim):
    tiles = split_up(shard, dim, lax.axis_size(axis))
    arrived = lax.all_to_all(tiles, axis, split_axis=0, concat_axis=0, tiled=True)
    return arrived.sum(axis=0)


def sum_in_two_steps(shard, axes, dim):
    far, near = axes
    tiles = split_up(shard, dim, lax.axis_size(far))
    nearer = sent_and_summed(tiles, near, dim + 1)
    arrived = lax.all_to_all(nearer, far, split_axis=0, concat_axis=0, tiled=True)
    return arrived.sum(axis=0)


def total_of(shard, axes):
    lines = shard.reshape(-1, shard.shape[-1])
    padded = rows_for(lines, lax.axis_size(axes[0]) * lax.axis_size(axes[1]))
    whole = gathered_by_axis(sum_in_two_steps(padded, axes, 0), axes, 0)
    return lax.slice_in_dim(whole, 0, len(lines)).reshape(shard.shape)


def of_everyone(shard, axis):
    return copy_for_each(shard, axis).max(axis=0)


def of_everyone_2(shard, axis):
    return copy_for_each(shard, axis).sum(axis=0)


def reduced_to_own(tiles, axes, order):
    lengths = [lax.axis_size(a) for a in axes]
    tiles = tiles.reshape(*lengths, *tiles.shape[1:])
    tiles = tiles.transpose(*order, *range(len(axes), tiles.ndim))
    tiles = tiles.reshape(-1, *tiles.shape[len(axes) :])
    for k in order:
        tiles = lax.psum_scatter(tiles, axes[k], scatter_dimension=0, tiled=True)
    return tiles[0]


def scatter_axes(shard, axes, order, dim):
    devices = lax.axis_size(axes)
    return reduced_to_own(split_up(shard, dim, devices), axes, order)


def join_stats(left_stats, right_stats):
    larger = jnp.maximum(left_stats[0], right_stats[0])
    summed = left_stats[1] * jnp.exp(left_stats[0] - larger) + right_stats[1] * jnp.exp(
        right_stats[0] - larger
    )
    return (larger, summed)


def shards(tokens, router, w_in, w_out):
    local_columns = router.shape[1]
    local_experts = local_columns // SLOTS
    seq_count = tokens.shape[0]
    width = tokens.shape[2]
    router_logits = jnp.einsum("bnq,qt->bnt", tokens, router, preferred_element_type=jnp.float32)
    local_max = jnp.max(router_logits, axis=1)
    local_total = jnp.sum(jnp.exp(router_logits - local_max[:, None, :]), axis=1)
    column_top, column_sum = merged((local_max, local_total), SEQ, join_stats)
    dispatch_weights = (
        jnp.exp(router_logits - column_top[:, None, :]) / column_sum[:, None, :]
    ).astype(jnp.bfloat16)
    partial_slot_sums = jnp.einsum(
        "mja,mjo->mao", dispatch_weights, tokens, preferred_element_type=jnp.float32
    )
    slot_input_rows = total_of(partial_slot_sums, (("seq_0", "seq_1"), "seq_2")).astype(
        jnp.bfloat16
    )
    split_count = lax.axis_size(SEQ) // local_experts
    own_expert = lax.axis_index(SEQ) // split_count
    own_input = lax.dynamic_slice_in_dim(slot_input_rows, own_expert * SLOTS, SLOTS, 1).reshape(
        seq_count * SLOTS, width
    )
    pre_active = jnp.dot(own_input, w_in[0], preferred_element_type=jnp.float32)
    hidden = jax.nn.gelu(pre_active, approximate=True).astype(jnp.bfloat16)
    piece_output = jnp.dot(hidden, w_out[0], preferred_element_type=jnp.float32).reshape(
        seq_count, 1, SLOTS, width
    )
    expert_mask = (jnp.arange(local_experts, dtype=jnp.int32) == own_expert).astype(jnp.float32)
    placed = (piece_output * expert_mask[None, :, None, None]).reshape(
        seq_count, local_columns, width
    )
    slot_output_rows = total_of(placed, (("seq_0", "seq_1"), "seq_2")).astype(jnp.bfloat16)
    row_top = of_everyone(jnp.max(router_logits, axis=2), EXP)
    row_exp = jnp.exp(router_logits - row_top[:, :, None])
    row_sum = of_everyone_2(jnp.sum(row_exp, axis=2), EXP)
    combine_weights = (row_exp / row_sum[:, :, None]).astype(jnp.bfloat16)
    token_partial = jnp.einsum(
        "ptx,pxg->ptg", combine_weights, slot_output_rows, preferred_element_type=jnp.float32
    )
    return scatter_axes(token_partial, EXP, (1, 0), 1).astype(jnp.bfloat16)


def solution(mesh):
    torus = Mesh(mesh.devices.reshape(4, 4, 2, 4, 4), ("seq_0", "seq_1", "seq_2", "exp_0", "exp_1"))
    placed = (P(None, SEQ, None), P(None, EXP), P(EXP_SEQ, None, None), P(EXP_SEQ, None, None))
    return jax.shard_map(
        shards, mesh=torus, in_specs=placed, out_specs=P(None, SEQ_EXP, None), check_vma=False
    )
```

profile of v0, /device:TPU:1, one launch (start us, length us, event | category | flops | bytes accessed | tf_op | source)
XLA Modules:
  0.0 291.5 jit_solution(15841729794630907802)
XLA Ops:
  6.5 0.0 copy-start
  6.5 1.6 copy-done
  8.1 1.7 fusion.27
  9.9 31.9 %all_to_all.55 = f32[16,2,512]{2,1,0:T(2,128)S(1)} all-to-all(f32[16,2,512]{2,1,0:T(2,128)S(1)} %broadcast_in_dim.25), channel_id=1, replica_groups=mesh['seq_0'=4,'seq_1'=4,'seq_2'=2,'exp_0'=4,'exp_1'=4] {'exp_0','exp_1'}, dimensions={0} | all-to-all | bytes 131072 | tf_op jit(solution)/shard_map/all_to_all | solution.py:16
  41.9 0.4 fusion.4
  42.3 15.4 %all_to_all.56 = f32[32,4,128]{2,1,0:T(4,128)S(1)} all-to-all(f32[32,4,128]{2,1,0:T(4,128)S(1)} %broadcast_in_dim.27), channel_id=1, replica_groups=mesh['seq_0'=4,'seq_1'=4,'seq_2'=2,'exp_0'=4,'exp_1'=4] {'seq_0','seq_1'..., dimensions={0} | all-to-all | bytes 131072 | tf_op jit(solution)/shard_map/all_to_all | solution.py:16
  57.9 0.5 fusion.6
  58.4 0.1 copy.40
  58.4 5.4 %all_to_all.57 = f32[2,16,8,1024]{3,2,1,0:T(8,128)} all-to-all(f32[2,16,8,1024]{3,2,1,0:T(8,128)S(1)} %bitcast.54), channel_id=1, replica_groups=mesh['seq_0'=4,'seq_1'=4,'seq_2'=2,'exp_0'=4,'exp_1'=4] {'seq_2'}, dimensions={0} | all-to-all | bytes 2097152 | tf_op jit(solution)/shard_map/all_to_all | solution.py:75
  63.9 1.3 reduce_sum.66
  65.2 19.2 %all_to_all.58 = f32[16,8,1024]{2,1,0:T(8,128)} all-to-all(f32[16,8,1024]{2,1,0:T(8,128)S(1)} %reduce_sum.66), channel_id=1, replica_groups=mesh['seq_0'=4,'seq_1'=4,'seq_2'=2,'exp_0'=4,'exp_1'=4] {'seq_0','seq_1'}, dimensions={0} | all-to-all | bytes 1048576 | tf_op jit(solution)/shard_map/all_to_all | solution.py:83
  84.4 1.1 reduce_sum.67
  85.5 0.7 broadcast_in_dim.28
  86.2 3.9 %all-to-all-start.5 = ((bf16[16,8,1024]{2,1,0:T(8,128)(2,1)}), bf16[16,8,1024]{2,1,0:T(8,128)(2,1)S(1)}, u32[]{:S(2)}, u32[]{:S(2)}) async-start(bf16[16,8,1024]{2,1,0:T(8,128)(2,1)} %broadcast_in_dim.28), calls=%async_computation.5 | async-start | bytes 524288 | tf_op jit(solution)/shard_map/all_to_all | solution.py:16
  90.2 0.1 mul.103
  90.3 9.8 %all-to-all-done.5 = bf16[16,8,1024]{2,1,0:T(8,128)(2,1)S(1)} async-done(((bf16[16,8,1024]{2,1,0:T(8,128)(2,1)}), bf16[16,8,1024]{2,1,0:T(8,128)(2,1)S(1)}, u32[]{:S(2)}, u32[]{:S(2)}) %all-to-all-start.5) | async-done | bytes 262176 | tf_op jit(solution)/shard_map/all_to_all | solution.py:16
  100.1 0.0 copy-start.2
  100.1 0.0 copy-start.1
  100.1 0.1 broadcast_in_dim.29
  100.1 5.8 %all_to_all.59 = bf16[2,16,8,1024]{3,2,1,0:T(8,128)(2,1)S(1)} all-to-all(bf16[2,16,8,1024]{3,2,1,0:T(8,128)(2,1)S(1)} %broadcast_in_dim.29), channel_id=1, replica_groups=mesh['seq_0'=4,'seq_1'=4,'seq_2'=2,'exp_0'=4,'exp_1'=4] {'seq_2'}, dimensions={0} | all-to-all | bytes 1048576 | tf_op jit(solution)/shard_map/all_to_all | solution.py:16
  106.0 0.0 copy-done.2
  106.1 0.3 fusion.22
  106.4 0.0 copy-done.1
  106.4 0.3 fusion
  106.7 0.1 mul.100
  106.8 0.1 multiply_bitcast_fusion
  106.9 0.1 copy.31
  107.0 5.4 %all_to_all.60 = f32[2,16,8,1024]{3,2,1,0:T(8,128)} all-to-all(f32[2,16,8,1024]{3,2,1,0:T(8,128)S(1)} %copy.31), channel_id=1, replica_groups=mesh['seq_0'=4,'seq_1'=4,'seq_2'=2,'exp_0'=4,'exp_1'=4] {'seq_2'}, dimensions={0} | all-to-all | bytes 2097152 | tf_op jit(solution)/shard_map/all_to_all | solution.py:75
  112.4 2.2 reduce_sum.68
  114.6 19.5 %all_to_all.61 = f32[16,8,1024]{2,1,0:T(8,128)S(1)} all-to-all(f32[16,8,1024]{2,1,0:T(8,128)} %reduce_sum.68), channel_id=1, replica_groups=mesh['seq_0'=4,'seq_1'=4,'seq_2'=2,'exp_0'=4,'exp_1'=4] {'seq_0','seq_1'}, dimensions={0} | all-to-all | bytes 1048576 | tf_op jit(solution)/shard_map/all_to_all | solution.py:83
  134.0 0.6 broadcast_in_dim.26
  134.7 3.5 %all-to-all-start.1 = ((f32[16,2,512]{2,1,0:T(2,128)}), f32[16,2,512]{2,1,0:T(2,128)S(1)}, u32[]{:S(2)}, u32[]{:S(2)}) async-start(f32[16,2,512]{2,1,0:T(2,128)} %broadcast_in_dim.26), calls=%async_computation.1 | async-start | bytes 131072 | tf_op jit(solution)/shard_map/all_to_all | solution.py:16
  138.2 13.8 %all-to-all-done.1 = f32[16,2,512]{2,1,0:T(2,128)S(1)} async-done(((f32[16,2,512]{2,1,0:T(2,128)}), f32[16,2,512]{2,1,0:T(2,128)S(1)}, u32[]{:S(2)}, u32[]{:S(2)}) %all-to-all-start.1) | async-done | bytes 65568 | tf_op jit(solution)/shard_map/all_to_all | solution.py:16
  152.0 0.7 broadcast_in_dim.30
  152.7 3.9 %all-to-all-start.9 = ((bf16[16,8,1024]{2,1,0:T(8,128)(2,1)}), bf16[16,8,1024]{2,1,0:T(8,128)(2,1)S(1)}, u32[]{:S(2)}, u32[]{:S(2)}) async-start(bf16[16,8,1024]{2,1,0:T(8,128)(2,1)} %broadcast_in_dim.30), calls=%async_computation.9 | async-start | bytes 524288 | tf_op jit(solution)/shard_map/all_to_all | solution.py:16
  156.7 0.0 reduce-scatter.3.cloned.1.call-start
  156.8 8.2 %all-to-all-done.9 = bf16[16,8,1024]{2,1,0:T(8,128)(2,1)S(1)} async-done(((bf16[16,8,1024]{2,1,0:T(8,128)(2,1)}), bf16[16,8,1024]{2,1,0:T(8,128)(2,1)S(1)}, u32[]{:S(2)}, u32[]{:S(2)}) %all-to-all-start.9) | async-done | bytes 262176 | tf_op jit(solution)/shard_map/all_to_all | solution.py:16
  165.0 0.1 broadcast_in_dim.31
  165.0 7.4 %all_to_all.62 = bf16[2,16,8,1024]{3,2,1,0:T(8,128)(2,1)S(1)} all-to-all(bf16[2,16,8,1024]{3,2,1,0:T(8,128)(2,1)S(1)} %broadcast_in_dim.31), channel_id=1, replica_groups=mesh['seq_0'=4,'seq_1'=4,'seq_2'=2,'exp_0'=4,'exp_1'=4] {'seq_2'}, dimensions={0} | all-to-all | bytes 1048576 | tf_op jit(solution)/shard_map/all_to_all | solution.py:16
  172.4 0.8 fusion.5
  173.2 2.2 copy.33
  175.4 0.0 reduce-scatter.3.cloned.1.call-update
  175.5 0.0 reduce-scatter.5.cloned.1.call-start
  175.5 43.3 %reduce-scatter.3.cloned.1.call-done = f32[4,2,32,1024]{3,2,1,0:T(8,128)} async-done(((f32[16,2,32,1024]{3,2,1,0:T(8,128)}), f32[4,2,32,1024]{3,2,1,0:T(8,128)}) %reduce-scatter.3.cloned.1.call-update) | async-done | bytes 1048592 | tf_op jit(solution)/shard_map/reduce_scatter | solution.py:108
  218.9 0.0 reduce-scatter.5.cloned.1.call-update
  218.9 64.1 %reduce-scatter.5.cloned.1.call-done = f32[1,2,32,1024]{3,2,1,0:T(8,128)} async-done(((f32[4,2,32,1024]{3,2,1,0:T(8,128)}), f32[1,2,32,1024]{3,2,1,0:T(8,128)}) %reduce-scatter.5.cloned.1.call-update) | async-done | bytes 262160 | tf_op jit(solution)/shard_map/reduce_scatter | solution.py:108
  283.0 1.6 convert_bitcast_fusion.1
  (17 shorter events, 0.4 us)
Async XLA Ops:
  6.5 1.6 copy-start
  86.2 13.8 %all-to-all-start.5 = ((bf16[16,8,1024]{2,1,0:T(8,128)(2,1)}), bf16[16,8,1024]{2,1,0:T(8,128)(2,1)S(1)}, u32[]{:S(2)}, u32[]{:S(2)}) async-start(bf16[16,8,1024]{2,1,0:T(8,128)(2,1)} %broadcast_in_dim.28), calls=%async_computation.5 | async-start | bytes 524288 | tf_op jit(solution)/shard_map/all_to_all | solution.py:16
  100.1 6.0 %copy-start.2 = (bf16[1,1024,512]{2,1,0:T(8,128)(2,1)S(1)}, bf16[1,1024,512]{2,1,0:T(8,128)(2,1)}, u32[]{:S(2)}) copy-start(bf16[1,1024,512]{2,1,0:T(8,128)(2,1)} %param.6) | copy-start | bytes 3145732
  100.1 6.3 %copy-start.1 = (bf16[1,512,1024]{2,1,0:T(8,128)(2,1)S(1)}, bf16[1,512,1024]{2,1,0:T(8,128)(2,1)}, u32[]{:S(2)}) copy-start(bf16[1,512,1024]{2,1,0:T(8,128)(2,1)} %param.7) | copy-start | bytes 3145732
  134.7 17.3 %all-to-all-start.1 = ((f32[16,2,512]{2,1,0:T(2,128)}), f32[16,2,512]{2,1,0:T(2,128)S(1)}, u32[]{:S(2)}, u32[]{:S(2)}) async-start(f32[16,2,512]{2,1,0:T(2,128)} %broadcast_in_dim.26), calls=%async_computation.1 | async-start | bytes 131072 | tf_op jit(solution)/shard_map/all_to_all | solution.py:16
  152.7 12.2 %all-to-all-start.9 = ((bf16[16,8,1024]{2,1,0:T(8,128)(2,1)}), bf16[16,8,1024]{2,1,0:T(8,128)(2,1)S(1)}, u32[]{:S(2)}, u32[]{:S(2)}) async-start(bf16[16,8,1024]{2,1,0:T(8,128)(2,1)} %broadcast_in_dim.30), calls=%async_computation.9 | async-start | bytes 524288 | tf_op jit(solution)/shard_map/all_to_all | solution.py:16
  156.7 62.2 %reduce-scatter.3.cloned.1.call-start = ((), (), s32[]{:S(2)}) async-start(), calls=%async_computation.13 | async-start | bytes 5242880 | tf_op jit(solution)/shard_map/reduce_scatter | solution.py:108
  175.5 107.5 %reduce-scatter.5.cloned.1.call-start = ((), (), s32[]{:S(2)}) async-start(), calls=%async_computation.14 | async-start | bytes 1310720 | tf_op jit(solution)/shard_map/reduce_scatter | solution.py:108
Sparse Core Ops, SparseCore 0:
  175.6 43.2 reduce-scatter.2
  221.7 61.2 reduce-scatter.4
where the time goes:
time: 292 us; the launch traced here: 291 us
  waiting for transfers between devices  139 us (48%)
  blocking collectives  110 us (38%)
  between operations  13.6 us (5%)
  starting transfers between devices  11.4 us (4%)
  other arithmetic  6.93 us (2%)
  local copies, waits for them, and re-layouts  6.54 us (2%)
  matrix products  3.61 us (1%)
    reduce_scatter x2, waiting for transfers between devices, reduced_to_own(): tiles = lax.psum_scatter(tiles, axes[k], scatter_dimension=0, tiled=True)  107 us
    all_to_all x4, blocking collectives, copy_for_each(): return lax.all_to_all(copies, axis, split_axis=0, concat_axis=0, tiled=True)  60.6 us
    all_to_all x2, blocking collectives, sum_in_two_steps(): lax.all_to_all(nearer, far, split_axis=0, concat_axis=0, tiled=True)  38.7 us
    all_to_all x3, waiting for transfers between devices, copy_for_each(): return lax.all_to_all(copies, axis, split_axis=0, concat_axis=0, tiled=True)  31.8 us
    all_to_all x3, starting transfers between devices, copy_for_each(): return lax.all_to_all(copies, axis, split_axis=0, concat_axis=0, tiled=True)  11.4 us
    all_to_all x2, blocking collectives, sent_and_summed(): lax.all_to_all(tiles, axis, split_axis=0, concat_axis=0, tiled=True)  10.8 us
  transfers between devices with their start and end apart: 5, of which 5 were waited for; matrix products, arithmetic and copies ran while one was open for 0% of the time, Pallas kernels for 0%

commit v1 on v0

v1 whole, which is shorter than its diff:
```python
import jax
import jax.numpy as jnp
from jax import lax
from jax.sharding import Mesh
from jax.sharding import PartitionSpec as P

SLOTS = 16
AXES = ("x", "zla", "zlb", "c", "zh", "y")
SEQ = ("x", "zla", "zlb", "c")
EXP = ("zh", "y")
f32, bf16 = jnp.float32, jnp.bfloat16


def swap(tiles, axis):
    return lax.all_to_all(tiles, axis, split_axis=0, concat_axis=0, tiled=True)


def in_three(v):
    hi = lax.reduce_precision(v, 8, 7)
    mid = lax.reduce_precision(v - hi, 8, 7)
    return [hi, mid, v - hi - mid]


def columns(parts, width=128):
    both = jnp.concatenate(parts, axis=-1)
    spare = [(0, 0)] * (both.ndim - 1) + [(0, width - both.shape[-1])]
    return jnp.pad(both, spare).astype(bf16)


def whole(cols):
    cols = cols.astype(f32)
    top = cols[..., 0:1] + cols[..., 1:2] + cols[..., 2:3]
    total = cols[..., 3:4] + cols[..., 4:5] + cols[..., 5:6]
    return top, total


def blend(rows, axis):
    width = rows.shape[-1] - 128
    top, total = whole(rows[..., width:])
    share = total * jnp.exp(top - top.max(axis=axis, keepdims=True))
    share = share / share.sum(axis=axis, keepdims=True)
    return (rows[..., :width].astype(f32) * share).sum(axis=axis).astype(bf16)


def shards(tokens, router, w_in, w_out):
    slots = router.shape[1]
    experts = slots // SLOTS
    width = tokens.shape[2]
    each = tokens.shape[1]
    nx, nzla, nzlb, nc, nzh, ny = (lax.axis_size(a) for a in AXES)
    chunk = each // nzh

    with jax.named_scope("tokens_c"):
        own = swap(tokens, "c")
        flat = own.reshape(nc * each, width)
        pair = [(0, 1), (1, 0)]
        w_in2 = lax.ppermute(w_in, "c", pair)
        w_out2 = lax.ppermute(w_out, "c", pair)

    with jax.named_scope("logits"):
        logits = jnp.einsum("dn,td->nt", router, flat, preferred_element_type=f32)
        top = logits.max(axis=1, keepdims=True)
        e1 = jnp.exp(logits - top)
        total = e1.sum(axis=1, keepdims=True)
        part = jnp.dot(e1.astype(bf16), flat, preferred_element_type=f32) / total
        stats = columns(in_three(top) + in_three(total))
        send = jnp.concatenate([part.astype(bf16), stats], axis=1)
        send = send.reshape(nx * nzla, 1, SLOTS, width + 128)
        send = jnp.broadcast_to(send, (nx * nzla, nzlb, SLOTS, width + 128))
        send = send.reshape(-1, SLOTS, width + 128)

    with jax.named_scope("slots_xzl"):
        arrived = swap(send, ("x", "zla", "zlb"))

    with jax.named_scope("ffn"):
        rows = blend(arrived, 0)
        out = 0.0
        for a, b in ((w_in, w_out), (w_in2, w_out2)):
            hidden = jnp.dot(rows, a[0], preferred_element_type=f32)
            hidden = jax.nn.gelu(hidden, approximate=True).astype(bf16)
            out = out + jnp.dot(hidden, b[0], preferred_element_type=f32)
        out = out.astype(bf16)

    with jax.named_scope("out_zl"):
        got = swap(jnp.broadcast_to(out, (nzla * nzlb, *out.shape)), ("zla", "zlb"))
        got = got.reshape(nzla, nzlb, SLOTS, width).astype(f32).sum(axis=1).astype(bf16)

    with jax.named_scope("row_exp"):
        m2 = logits.max(axis=0, keepdims=True)
        e2 = jnp.exp(logits - m2).astype(bf16)
        e2 = e2.reshape(slots, nc, nzh, chunk).transpose(2, 1, 0, 3)
        m2 = jnp.concatenate(in_three(m2), axis=0).reshape(3, nc, nzh, chunk)
        m2 = jnp.pad(m2.transpose(2, 1, 0, 3), ((0, 0), (0, 0), (0, 5), (0, 0)))
        row = jnp.concatenate(
            [
                e2.reshape(nzh, nc * slots, chunk),
                m2.astype(bf16).reshape(nzh, nc * 8, chunk),
                jnp.broadcast_to(got.reshape(1, -1, chunk), (nzh, got.size // chunk, chunk)),
            ],
            axis=1,
        )

    with jax.named_scope("out_zh"):
        row = swap(row, "zh")

    with jax.named_scope("out_x"):
        at = nc * slots + nc * 8
        found = row[:, at:].reshape(nzh, nzla * SLOTS, width)
        found = swap(jnp.broadcast_to(found, (nx, *found.shape)), "x")

    with jax.named_scope("mix"):
        e2 = row[:, : nc * slots].reshape(nzh, nc, slots, chunk).astype(f32)
        m2 = row[:, nc * slots : at].reshape(nzh, nc, 8, chunk).astype(f32)
        m2 = m2[:, :, 0] + m2[:, :, 1] + m2[:, :, 2]
        top = m2.max(axis=0)
        e2 = e2 * jnp.exp(m2 - top)[:, :, None, :]
        total = e2.sum(axis=(0, 2))
        mix = (e2 / total[None, :, None, :]).astype(bf16)
        mix = mix.reshape(nzh, nc, nx, nzla * SLOTS, chunk)
        out = jnp.einsum("zcxrt,xzrg->ctg", mix, found, preferred_element_type=f32)
        stats = columns([s[:, :, None] for s in in_three(top) + in_three(total)])
        out = jnp.concatenate([out.astype(bf16), stats], axis=2)
        out = out.reshape(nc * ny, chunk // ny, width + 128)

    with jax.named_scope("out_cy"):
        out = swap(out, ("c", "y")).reshape(nc, ny, chunk // ny, width + 128)

    with jax.named_scope("last"):
        return blend(out, 1)


def solution(mesh):
    torus = Mesh(mesh.devices.reshape(4, 2, 2, 2, 4, 4), AXES)
    placed = (P(None, SEQ, None), P(None, EXP), P(EXP + SEQ, None, None), P(EXP + SEQ, None, None))
    return jax.shard_map(
        shards, mesh=torus, in_specs=placed, out_specs=P(None, SEQ + EXP, None), check_vma=False
    )
```

time: 292 us -> 135 us (0.46)
  the two profiles are of different devices: /device:TPU:1 before, /device:TPU:33 now
where the time goes in v1:
time: 135 us; the launch traced here: 134 us
  blocking collectives  67.8 us (50%)
  waiting for transfers between devices  24.7 us (18%)
  starting transfers between devices  23.1 us (17%)
  local copies, waits for them, and re-layouts  8.23 us (6%)
  other arithmetic  5.58 us (4%)
  matrix products  4.48 us (3%)
    all_to_all x3, blocking collectives, swap(): return lax.all_to_all(tiles, axis, split_axis=0, concat_axis=0, tiled=True)  67.8 us
    all_to_all x3, waiting for transfers between devices, swap(): return lax.all_to_all(tiles, axis, split_axis=0, concat_axis=0, tiled=True)  24.7 us
    all_to_all x3, starting transfers between devices, swap(): return lax.all_to_all(tiles, axis, split_axis=0, concat_axis=0, tiled=True)  18.6 us
    reduce_sum x2, other arithmetic, blend(): return (rows[..., :width].astype(f32) * share).sum(axis=axis).astype(bf16)  3.9 us
  transfers between devices with their start and end apart: 5, of which 3 were waited for; matrix products, arithmetic and copies ran while one was open for 3% of the time, Pallas kernels for 0%

profile of v1, /device:TPU:33, one launch (start us, length us, event | category | flops | bytes accessed | tf_op | source)
XLA Modules:
  0.0 134.2 jit_solution(18184577732145790403)
XLA Ops:
  0.0 0.0 copy-start
  0.0 7.0 %all_to_all.30 = bf16[2,512,1024]{2,1,0:T(8,128)(2,1)S(1)} all-to-all(bf16[2,512,1024]{2,1,0:T(8,128)(2,1)} %param.4), channel_id=1, replica_groups=mesh['x'=4,'zla'=2,'zlb'=2,'c'=2,'zh'=4,'y'=4] {'c'}, dimensions={0} | all-to-all | bytes 4194304 | tf_op jit(solution)/shard_map/tokens_c/all_to_all | solution.py:15
  7.1 0.0 copy-done
  7.1 0.9 fusion.96
  8.0 0.2 fusion.90
  8.2 0.5 fusion.1
  8.7 0.0 copy-start.1
  8.7 0.0 copy-start.2
  8.8 0.1 copy.51
  9.0 0.9 broadcast_in_dim.13
  9.8 8.5 %all-to-all-start.1 = ((bf16[16,16,1152]{2,1,0:T(8,128)(2,1)}), bf16[16,16,1152]{2,1,0:T(8,128)(2,1)S(1)}, u32[]{:S(2)}, u32[]{:S(2)}) async-start(bf16[16,16,1152]{2,1,0:T(8,128)(2,1)} %bitcast.9), calls=%async_computation.1 | async-start | bytes 1179648 | tf_op jit(solution)/shard_map/slots_xzl/all_to_all | solution.py:15
  18.4 0.0 copy-done.1
  18.4 2.6 %collective-permute-start = (bf16[1,1024,512]{2,1,0:T(8,128)(2,1)S(1)}, bf16[1,1024,512]{2,1,0:T(8,128)(2,1)}, u32[]{:S(2)}, u32[]{:S(2)}) collective-permute-start(bf16[1,1024,512]{2,1,0:T(8,128)(2,1)S(1)} %copy-done.1), channel_id=1, source_target_pairs={{0,16},{16,0},{1,17},{17,1},{2,18},{18,2},{3,19},{19,3},{4,20},{20... | collective-permute-start | bytes 3145736 | tf_op jit(solution)/shard_map/tokens_c/ppermute | solution.py:57
  21.0 0.0 copy-done.2
  21.0 1.9 %collective-permute-start.1 = (bf16[1,512,1024]{2,1,0:T(8,128)(2,1)S(1)}, bf16[1,512,1024]{2,1,0:T(8,128)(2,1)}, u32[]{:S(2)}, u32[]{:S(2)}) collective-permute-start(bf16[1,512,1024]{2,1,0:T(8,128)(2,1)S(1)} %copy-done.2), channel_id=1, source_target_pairs={{0,16},{16,0},{1,17},{17,1},{2,18},{18,2},{3,19},{19,3},{4,20},{20... | collective-permute-start | bytes 3145736 | tf_op jit(solution)/shard_map/tokens_c/ppermute | solution.py:58
  22.9 0.8 exponential_convert_fusion
  23.7 1.1 reshape.220
  24.8 0.7 copy.49
  25.5 7.1 %all-to-all-done.1 = bf16[16,16,1152]{2,1,0:T(8,128)(2,1)S(1)} async-done(((bf16[16,16,1152]{2,1,0:T(8,128)(2,1)}), bf16[16,16,1152]{2,1,0:T(8,128)(2,1)S(1)}, u32[]{:S(2)}, u32[]{:S(2)}) %all-to-all-start.1) | async-done | bytes 589856 | tf_op jit(solution)/shard_map/slots_xzl/all_to_all | solution.py:15
  32.6 0.4 copy.52
  33.1 0.1 convert_element_type.74
  33.2 0.2 multiply_reduce_fusion.1
  33.4 0.2 copy.62
  33.6 0.5 fusion.8
  34.1 0.0 copy-start.3
  34.1 0.0 collective-permute-done
  34.1 0.0 collective-permute-done.1
  34.1 2.1 %fusion.3 = bf16[16,1024]{1,0:T(8,128)(2,1)S(1)} fusion(f32[16,1024]{1,0:T(8,128)S(1)} %fusion.8, bf16[1,512,1024]{2,1,0:T(8,128)(2,1)} %collective-permute-done.1, bf16[1,1024,512]{2,1,0:T(8,128)(2,1)} %collective-permute-done, bf16[16,1024]{0,1:T(8,128)(2,1)S(1)} %copy.62), kind=kOutput, calls=%fused_computation.8 | convolution fusion | flops 33660928 | bytes 2228224 | tf_op jit(solution)/shard_map/ffn/dot_general | solution.py:81
  36.2 0.7 broadcast_in_dim.14
  36.8 6.6 %all-to-all-start.2 = ((bf16[4,16,1024]{2,1,0:T(8,128)(2,1)}), bf16[4,16,1024]{2,1,0:T(8,128)(2,1)S(1)}, u32[]{:S(2)}, u32[]{:S(2)}) async-start(bf16[4,16,1024]{2,1,0:T(8,128)(2,1)} %broadcast_in_dim.14), calls=%async_computation.2 | async-start | bytes 262144 | tf_op jit(solution)/shard_map/out_zl/all_to_all | solution.py:15
  43.5 4.2 %all-to-all-done.2 = bf16[4,16,1024]{2,1,0:T(8,128)(2,1)S(1)} async-done(((bf16[4,16,1024]{2,1,0:T(8,128)(2,1)}), bf16[4,16,1024]{2,1,0:T(8,128)(2,1)S(1)}, u32[]{:S(2)}, u32[]{:S(2)}) %all-to-all-start.2) | async-done | bytes 131104 | tf_op jit(solution)/shard_map/out_zl/all_to_all | solution.py:15
  47.8 0.0 copy-done.3
  47.9 43.8 %all_to_all.31 = bf16[4,528,128]{2,1,0:T(8,128)(2,1)S(1)} all-to-all(bf16[4,528,128]{2,1,0:T(8,128)(2,1)S(1)} %pad_maximum_fusion), channel_id=1, replica_groups=mesh['x'=4,'zla'=2,'zlb'=2,'c'=2,'zh'=4,'y'=4] {'zh'}, dimensions={0} | all-to-all | bytes 1081344 | tf_op jit(solution)/shard_map/out_zh/all_to_all | solution.py:15
  91.7 0.1 slice_convert_fusion.1
  91.8 0.1 reshape.225
  91.9 1.1 broadcast_in_dim.17
  93.0 3.5 %all-to-all-start.4 = ((bf16[4,4,32,1024]{3,2,1,0:T(8,128)(2,1)}), bf16[4,4,32,1024]{3,2,1,0:T(8,128)(2,1)S(1)}, u32[]{:S(2)}, u32[]{:S(2)}) async-start(bf16[4,4,32,1024]{3,2,1,0:T(8,128)(2,1)} %broadcast_in_dim.17), calls=%async_computation.4 | async-start | bytes 2097152 | tf_op jit(solution)/shard_map/out_x/all_to_all | solution.py:15
  96.6 0.1 fusion.14
  96.7 0.1 copy.55
  96.8 13.3 %all-to-all-done.4 = bf16[4,4,32,1024]{3,2,1,0:T(8,128)(2,1)S(1)} async-done(((bf16[4,4,32,1024]{3,2,1,0:T(8,128)(2,1)}), bf16[4,4,32,1024]{3,2,1,0:T(8,128)(2,1)S(1)}, u32[]{:S(2)}, u32[]{:S(2)}) %all-to-all-start.4) | async-done | bytes 1048608 | tf_op jit(solution)/shard_map/out_x/all_to_all | solution.py:15
  110.2 0.5 fusion
  110.7 17.0 %all_to_all.32 = bf16[8,32,1152]{2,1,0:T(8,128)(2,1)S(1)} all-to-all(bf16[8,32,1152]{2,1,0:T(8,128)(2,1)S(1)} %bitcast.115), channel_id=1, replica_groups=mesh['x'=4,'zla'=2,'zlb'=2,'c'=2,'zh'=4,'y'=4] {'c','y'}, dimensions={0} | all-to-all | bytes 1179648 | tf_op jit(solution)/shard_map/out_cy/all_to_all | solution.py:15
  127.7 1.6 %copy.56 = bf16[8,32,1152]{1,0,2:T(8,128)(2,1)S(1)} copy(bf16[8,32,1152]{2,1,0:T(8,128)(2,1)S(1)} %all_to_all.32) | data formatting | bytes 1179648 | tf_op jit(solution)/shard_map/out_cy/all_to_all | solution.py:15
  129.3 0.1 slice_convert_fusion
  129.5 3.7 %multiply_reduce_fusion = bf16[2,32,1024]{1,0,2:T(2,128)(2,1)S(1)} fusion(bf16[2,4,32,1152]{2,1,0,3:T(4,128)(2,1)S(1)} %bitcast.112, f32[2,4,32]{2,1,0:T(4,128)S(1)} %divide_bitcast_fusion.1), kind=kLoop, calls=%fused_computation | loop fusion | flops 720896 | bytes 656384 | tf_op jit(solution)/shard_map/last/reduce_sum | solution.py:42
  133.2 1.0 copy.57
  (29 shorter events, 0.6 us)
Async XLA Ops:
  0.0 7.1 %copy-start = (bf16[1024,128]{1,0:T(8,128)(2,1)S(1)}, bf16[1024,128]{1,0:T(8,128)(2,1)}, u32[]{:S(2)}) copy-start(bf16[1024,128]{1,0:T(8,128)(2,1)} %param.5) | copy-start | bytes 786436
  8.7 9.7 %copy-start.1 = (bf16[1,1024,512]{2,1,0:T(8,128)(2,1)S(1)}, bf16[1,1024,512]{2,1,0:T(8,128)(2,1)}, u32[]{:S(2)}) copy-start(bf16[1,1024,512]{2,1,0:T(8,128)(2,1)} %param.6) | copy-start | bytes 3145732
  8.7 12.2 %copy-start.2 = (bf16[1,512,1024]{2,1,0:T(8,128)(2,1)S(1)}, bf16[1,512,1024]{2,1,0:T(8,128)(2,1)}, u32[]{:S(2)}) copy-start(bf16[1,512,1024]{2,1,0:T(8,128)(2,1)} %param.7) | copy-start | bytes 3145732
  9.8 22.8 %all-to-all-start.1 = ((bf16[16,16,1152]{2,1,0:T(8,128)(2,1)}), bf16[16,16,1152]{2,1,0:T(8,128)(2,1)S(1)}, u32[]{:S(2)}, u32[]{:S(2)}) async-start(bf16[16,16,1152]{2,1,0:T(8,128)(2,1)} %bitcast.9), calls=%async_computation.1 | async-start | bytes 1179648 | tf_op jit(solution)/shard_map/slots_xzl/all_to_all | solution.py:15
  18.4 15.7 %collective-permute-start = (bf16[1,1024,512]{2,1,0:T(8,128)(2,1)S(1)}, bf16[1,1024,512]{2,1,0:T(8,128)(2,1)}, u32[]{:S(2)}, u32[]{:S(2)}) collective-permute-start(bf16[1,1024,512]{2,1,0:T(8,128)(2,1)S(1)} %copy-done.1), channel_id=1, source_target_pairs={{0,16},{16,0},{1,17},{17,1},{2,18},{18,2},{3,19},{19,3},{4,20},{20... | collective-permute-start | bytes 3145736 | tf_op jit(solution)/shard_map/tokens_c/ppermute | solution.py:57
  21.0 13.1 %collective-permute-start.1 = (bf16[1,512,1024]{2,1,0:T(8,128)(2,1)S(1)}, bf16[1,512,1024]{2,1,0:T(8,128)(2,1)}, u32[]{:S(2)}, u32[]{:S(2)}) collective-permute-start(bf16[1,512,1024]{2,1,0:T(8,128)(2,1)S(1)} %copy-done.2), channel_id=1, source_target_pairs={{0,16},{16,0},{1,17},{17,1},{2,18},{18,2},{3,19},{19,3},{4,20},{20... | collective-permute-start | bytes 3145736 | tf_op jit(solution)/shard_map/tokens_c/ppermute | solution.py:58
  34.1 13.8 %copy-start.3 = (bf16[128,2,4,128]{3,0,1,2:T(8,128)(2,1)S(1)}, bf16[128,2,4,128]{3,0,1,2:T(8,128)(2,1)}, u32[]{:S(2)}) copy-start(bf16[128,2,4,128]{3,0,1,2:T(8,128)(2,1)} %copy.49) | copy-start | bytes 786436
  36.8 10.9 %all-to-all-start.2 = ((bf16[4,16,1024]{2,1,0:T(8,128)(2,1)}), bf16[4,16,1024]{2,1,0:T(8,128)(2,1)S(1)}, u32[]{:S(2)}, u32[]{:S(2)}) async-start(bf16[4,16,1024]{2,1,0:T(8,128)(2,1)} %broadcast_in_dim.14), calls=%async_computation.2 | async-start | bytes 262144 | tf_op jit(solution)/shard_map/out_zl/all_to_all | solution.py:15
  93.0 17.1 %all-to-all-start.4 = ((bf16[4,4,32,1024]{3,2,1,0:T(8,128)(2,1)}), bf16[4,4,32,1024]{3,2,1,0:T(8,128)(2,1)S(1)}, u32[]{:S(2)}, u32[]{:S(2)}) async-start(bf16[4,4,32,1024]{3,2,1,0:T(8,128)(2,1)} %broadcast_in_dim.17), calls=%async_computation.4 | async-start | bytes 2097152 | tf_op jit(solution)/shard_map/out_x/all_to_all | solution.py:15

commit v2 on v1

v2 whole, which is shorter than its diff:
```python
import functools

import jax
import jax.numpy as jnp
from jax import lax
from jax.experimental import pallas as pl
from jax.experimental.pallas import tpu as pltpu
from jax.sharding import Mesh
from jax.sharding import PartitionSpec as P

SLOTS = 16
LANES = 128
AXES = ("x", "zla", "zlb", "c", "zh", "y")
SEQ = ("x", "zla", "zlb", "c")
EXP = ("zh", "y")
f32, bf16 = jnp.float32, jnp.bfloat16


def swap(tiles, axis):
    return lax.all_to_all(tiles, axis, split_axis=0, concat_axis=0, tiled=True)


def in_three(v):
    hi = v.astype(bf16).astype(f32)
    mid = (v - hi).astype(bf16).astype(f32)
    return [hi, mid, v - hi - mid]


def as_columns(parts):
    lane = lax.broadcasted_iota(jnp.int32, (parts[0].shape[0], LANES), 1)
    out = jnp.zeros(lane.shape, f32)
    for k, part in enumerate(parts):
        out = jnp.where(lane == k, part, out)
    return out.astype(bf16)


def blend(ref, pieces):
    width = ref.shape[-1] - LANES
    tops, totals = [], []
    for k in pieces:
        cols = ref[(*k, slice(None), slice(width, width + LANES))].astype(f32)
        tops.append(cols[:, 0:1] + cols[:, 1:2] + cols[:, 2:3])
        totals.append(cols[:, 3:4] + cols[:, 4:5] + cols[:, 5:6])
    top = functools.reduce(jnp.maximum, tops)
    shares = [s * jnp.exp(t - top) for t, s in zip(tops, totals)]
    scale = 1.0 / functools.reduce(jnp.add, shares)
    out = 0.0
    for k, share in zip(pieces, shares):
        out = out + ref[(*k, slice(None), slice(0, width))].astype(f32) * (share * scale)
    return out


def score_kernel(tok_ref, router_ref, send_ref, logit_ref):
    tok = tok_ref[...].reshape(-1, tok_ref.shape[-1])
    width = tok.shape[1]
    logits = jnp.dot(tok, router_ref[...], preferred_element_type=f32)
    logit_ref[...] = logits
    logits = logits.T
    top = logits.max(axis=1, keepdims=True)
    e1 = jnp.exp(logits - top)
    total = e1.sum(axis=1, keepdims=True)
    part = jnp.dot(e1.astype(bf16), tok, preferred_element_type=f32) * (1.0 / total)
    part = part.astype(bf16)
    stats = as_columns(in_three(top) + in_three(total))
    experts = logits.shape[0] // SLOTS
    copies = send_ref.shape[0] // experts
    for e in range(experts):
        for k in range(copies):
            send_ref[e * copies + k, :, 0:width] = part[e * SLOTS : (e + 1) * SLOTS]
            send_ref[e * copies + k, :, width:] = stats[e * SLOTS : (e + 1) * SLOTS]


def row_kernel(at_ref, logit_ref, *refs):
    outs, hold = refs[:-1], refs[-1]
    n, slots = len(outs), logit_ref.shape[1]
    cores = logit_ref.shape[0] // (n * LANES)
    per = LANES // n
    zero = jnp.zeros((1, LANES), f32)
    for y in range(n):
        rows = []
        for c in range(cores):
            at = [(c * n + z) * LANES + y * per for z in range(n)]
            logits = jnp.concatenate([logit_ref[i : i + per] for i in at], axis=0).T
            top = logits.max(axis=0, keepdims=True)
            hold[y, c * slots : (c + 1) * slots] = jnp.exp(logits - top).astype(bf16)
            rows += in_three(top) + [zero] * 5
        hold[y, cores * slots :] = jnp.concatenate(rows, axis=0).astype(bf16)
    for k in range(n):
        outs[k][...] = hold[(at_ref[0] + k) % n]


def ffn_kernel(got_ref, a_ref, a2_ref, b_ref, b2_ref, out_ref):
    rows = blend(got_ref, [(k,) for k in range(got_ref.shape[0])]).astype(bf16)
    out = 0.0
    for a, b in ((a_ref, b_ref), (a2_ref, b2_ref)):
        hidden = jnp.dot(rows, a[0], preferred_element_type=f32)
        hidden = jax.nn.gelu(hidden, approximate=True).astype(bf16)
        out = out + jnp.dot(hidden, b[0], preferred_element_type=f32)
    out = out.astype(bf16)
    for k in range(out_ref.shape[0]):
        out_ref[k] = out


def mix_kernel(at_ref, r0, r1, r2, r3, found_ref, out_ref):
    rs = (r0, r1, r2, r3)
    n, slots = len(rs), found_ref.shape[0] * found_ref.shape[2]
    width = found_ref.shape[-1]
    cores = r0.shape[0] // slots
    nz = out_ref.shape[0] // cores
    per = LANES // nz
    weights, stats = [[] for _ in rs], []
    for c in range(cores):
        tops = []
        for r in rs:
            m = r[cores * slots :].astype(f32)[8 * c : 8 * c + 8]
            tops.append(m[0:1] + m[1:2] + m[2:3])
        top = functools.reduce(jnp.maximum, tops)
        e2 = [
            r[c * slots : (c + 1) * slots].astype(f32) * jnp.exp(t - top)
            for r, t in zip(rs, tops)
        ]
        total = functools.reduce(jnp.add, [e.sum(axis=0, keepdims=True) for e in e2])
        scale = 1.0 / total
        for k in range(n):
            weights[k].append((e2[k] * scale).T.astype(bf16))
        zero = jnp.zeros((2, LANES), f32)
        rows = jnp.concatenate(in_three(top) + in_three(total) + [zero], axis=0)
        stats.append(rows.astype(bf16))
    out = 0.0
    for k in range(n):
        y = (at_ref[0] + n - k) % n
        block = found_ref[:, y].reshape(slots, width)
        out = out + jnp.dot(jnp.concatenate(weights[k], axis=0), block, preferred_element_type=f32)
    out = out.astype(bf16)
    for c in range(cores):
        for z in range(nz):
            at, to = c * LANES + z * per, c * nz + z
            for j in range(width // LANES):
                out_ref[to, j * per : (j + 1) * per] = out[at : at + per, j * LANES : (j + 1) * LANES]
            out_ref[to, width // LANES * per :] = stats[c]


def last_kernel(at_ref, got_ref, out_ref, hold):
    seqs, per, width = out_ref.shape
    n = got_ref.shape[0] // seqs
    end = width // LANES * per
    both = [got_ref[k, end:].astype(f32) for k in range(seqs * n)]
    both = both + [jnp.zeros((LANES - 8 * len(both), LANES), f32)]
    hold[...] = jnp.concatenate(both, axis=0).T
    cols = hold[pl.ds(at_ref[0] * per, per)]
    for s in range(seqs):
        tops, totals = [], []
        for k in range(n):
            i = 8 * (s * n + k)
            tops.append(cols[:, i : i + 1] + cols[:, i + 1 : i + 2] + cols[:, i + 2 : i + 3])
            totals.append(cols[:, i + 3 : i + 4] + cols[:, i + 4 : i + 5] + cols[:, i + 5 : i + 6])
        top = functools.reduce(jnp.maximum, tops)
        shares = [d * jnp.exp(t - top) for t, d in zip(tops, totals)]
        scale = 1.0 / functools.reduce(jnp.add, shares)
        shares = [v * scale for v in shares]
        for j in range(width // LANES):
            out = 0.0
            for k in range(n):
                out = out + got_ref[s * n + k, j * per : (j + 1) * per].astype(f32) * shares[k]
            out_ref[s, :, j * LANES : (j + 1) * LANES] = out.astype(bf16)


def call(kernel, outs, *args, scalar=False, scratch=()):
    kind = pltpu.MemorySpace.VMEM
    specs = [pl.BlockSpec(memory_space=kind) for _ in args]
    if scalar:
        specs[0] = pl.BlockSpec(memory_space=pltpu.MemorySpace.SMEM)
    return pl.pallas_call(
        kernel,
        out_shape=outs,
        in_specs=specs,
        out_specs=jax.tree.map(lambda _: pl.BlockSpec(memory_space=kind), outs),
        scratch_shapes=scratch,
        compiler_params=pltpu.CompilerParams(vmem_limit_bytes=40 << 20),
    )(*args)


def shape(*lengths, kind=bf16):
    return jax.ShapeDtypeStruct(lengths, kind)


def shards(tokens, router, w_in, w_out):
    slots = router.shape[1]
    width = tokens.shape[2]
    each = tokens.shape[1]
    nx, nzla, nzlb, nc, nzh, ny = (lax.axis_size(a) for a in AXES)
    assert each == nzh * LANES and slots == nx * nzla * SLOTS
    assert nzh == ny == nx
    here_y = lax.axis_index("y").astype(jnp.int32).reshape(1)
    here_zh = lax.axis_index("zh").astype(jnp.int32).reshape(1)
    per = LANES // nzh

    own = swap(tokens, "c")

    send, logits = call(
        score_kernel,
        (shape(nx * nzla * nzlb, SLOTS, width + LANES), shape(nc * each, slots, kind=f32)),
        own,
        router,
    )

    arrived = swap(send, ("x", "zla", "zlb"))

    pair = [(0, 1), (1, 0)]
    w_in2 = lax.ppermute(w_in, "c", pair)
    w_out2 = lax.ppermute(w_out, "c", pair)

    block = nc * (slots + 8)
    rows = call(
        row_kernel,
        (shape(block, LANES),) * ny,
        here_y,
        logits,
        scalar=True,
        scratch=(pltpu.VMEM((ny, block, LANES), bf16),),
    )

    rows = list(rows)
    for k in range(1, ny):
        rows[k] = lax.ppermute(rows[k], "y", [(i, (i + k) % ny) for i in range(ny)])

    out = call(ffn_kernel, shape(nzla * nzlb, SLOTS, width), arrived, w_in, w_in2, w_out, w_out2)

    got = swap(out, ("zla", "zlb"))
    got = got.reshape(nzla, nzlb, SLOTS, width).astype(f32).sum(axis=1).astype(bf16)
    got = got.reshape(nzla * SLOTS, width)

    found = swap(jnp.broadcast_to(got, (nx * ny, *got.shape)), ("x", "y"))
    found = found.reshape(nx, ny, *got.shape)

    block = width // LANES * per + 8
    out = call(mix_kernel, shape(nc * nzh, block, LANES), here_y, *rows, found, scalar=True)

    out = swap(out, ("c", "zh"))

    return call(
        last_kernel,
        shape(nc, per, width),
        here_zh,
        out,
        scalar=True,
        scratch=(pltpu.VMEM((LANES, LANES), f32),),
    )


def solution(mesh):
    torus = Mesh(mesh.devices.reshape(4, 2, 2, 2, 4, 4), AXES)
    placed = (P(None, SEQ, None), P(None, EXP), P(EXP + SEQ, None, None), P(EXP + SEQ, None, None))
    return jax.shard_map(
        shards, mesh=torus, in_specs=placed, out_specs=P(None, SEQ + EXP, None), check_vma=False
    )
```

time: 135 us -> 120 us (0.89)
  the two profiles are of different devices: /device:TPU:33 before, /device:TPU:1 now
where the time goes in v2:
time: 120 us; the launch traced here: 119 us
  waiting for transfers between devices  48.4 us (40%)
  starting transfers between devices  37.9 us (32%)
  blocking collectives  20.4 us (17%)
  Pallas kernels  6.93 us (6%)
  local copies, waits for them, and re-layouts  5.56 us (5%)
    all_to_all x3, waiting for transfers between devices, swap(): return lax.all_to_all(tiles, axis, split_axis=0, concat_axis=0, tiled=True)  39.1 us
    all_to_all x3, starting transfers between devices, swap(): return lax.all_to_all(tiles, axis, split_axis=0, concat_axis=0, tiled=True)  22.9 us
    all_to_all x2, blocking collectives, swap(): return lax.all_to_all(tiles, axis, split_axis=0, concat_axis=0, tiled=True)  20.4 us
    ppermute x3, starting transfers between devices, shards(): rows[k] = lax.ppermute(rows[k], 'y', [(i, (i + k) % ny) for i in range(ny)])  10.7 us
    ppermute x3, waiting for transfers between devices, shards(): rows[k] = lax.ppermute(rows[k], 'y', [(i, (i + k) % ny) for i in range(ny)])  7.75 us
    pallas_call x5, Pallas kernels, call(): pl.pallas_call(kernel, out_shape=outs, in_specs=specs, out_specs=jax.tree...  6.93 us
    unnamed x14, local copies, waits for them, and re-layouts  4.45 us
  transfers between devices with their start and end apart: 8, of which 6 were waited for; matrix products, arithmetic and copies ran while one was open for 0% of the time, Pallas kernels for 0%

profile of v2, /device:TPU:1, one launch (start us, length us, event | category | flops | bytes accessed | tf_op | source)
XLA Modules:
  0.0 119.2 jit_solution(1914873656931811751)
XLA Ops:
  0.0 0.0 copy-start.6
  0.0 13.2 %all_to_all.25.tok_ref = bf16[2,512,1024]{2,1,0:T(8,128)(2,1)S(1)} all-to-all(bf16[2,512,1024]{2,1,0:T(8,128)(2,1)} %param.4), channel_id=1, replica_groups=mesh['x'=4,'zla'=2,'zlb'=2,'c'=2,'zh'=4,'y'=4] {'c'}, dimensions={0} | all-to-all | bytes 4194304 | tf_op jit(solution)/shard_map/all_to_all | solution.py:20
  13.2 0.0 copy-done.6
  13.2 0.0 copy-start
  13.2 0.0 copy-start.1
  13.2 2.6 %shard_map.46 = (bf16[16,16,1152]{2,1,0:T(8,128)(2,1)}, f32[1024,128]{1,0:T(8,128)S(1)}) custom-call(bf16[2,512,1024]{2,1,0:T(8,128)(2,1)S(1)} %all_to_all.25.tok_ref, bf16[1024,128]{1,0:T(8,128)(2,1)S(1)} %copy-done.6), custom_call_target="tpu_custom_call" | custom-call | tf_op jit(solution)/shard_map/pallas_call | solution.py:173
  15.8 3.6 %all-to-all-start.1 = ((bf16[16,16,1152]{2,1,0:T(8,128)(2,1)}), bf16[16,16,1152]{2,1,0:T(8,128)(2,1)S(1)}, u32[]{:S(2)}, u32[]{:S(2)}) async-start(bf16[16,16,1152]{2,1,0:T(8,128)(2,1)} %get-tuple-element.16), calls=%async_computation.1 | async-start | bytes 1179648 | tf_op jit(solution)/shard_map/all_to_all | solution.py:20
  19.4 0.0 copy-done
  19.4 2.3 %collective-permute-start.3 = (bf16[1,1024,512]{2,1,0:T(8,128)(2,1)S(1)}, bf16[1,1024,512]{2,1,0:T(8,128)(2,1)S(1)}, u32[]{:S(2)}, u32[]{:S(2)}) collective-permute-start(bf16[1,1024,512]{2,1,0:T(8,128)(2,1)S(1)} %copy-done), channel_id=1, source_target_pairs={{0,16},{16,0},{1,17},{17,1},{2,18},{18,2},{3,19},{19,3},{4,20},{20... | collective-permute-start | bytes 3145736 | tf_op jit(solution)/shard_map/ppermute | solution.py:210
  21.7 0.0 copy-done.1
  21.7 2.0 %collective-permute-start.4 = (bf16[1,512,1024]{2,1,0:T(8,128)(2,1)S(1)}, bf16[1,512,1024]{2,1,0:T(8,128)(2,1)S(1)}, u32[]{:S(2)}, u32[]{:S(2)}) collective-permute-start(bf16[1,512,1024]{2,1,0:T(8,128)(2,1)S(1)} %copy-done.1), channel_id=1, source_target_pairs={{0,16},{16,0},{1,17},{17,1},{2,18},{18,2},{3,19},{19,3},{4,20},{20... | collective-permute-start | bytes 3145736 | tf_op jit(solution)/shard_map/ppermute | solution.py:211
  23.8 0.2 collective-permute-done.3.a2_ref
  24.0 0.0 copy-start.2
  24.0 1.0 copy-done.2
  25.0 1.3 %collective-permute-done.4.b2_ref = bf16[1,512,1024]{2,1,0:T(8,128)(2,1)S(1)} collective-permute-done((bf16[1,512,1024]{2,1,0:T(8,128)(2,1)S(1)}, bf16[1,512,1024]{2,1,0:T(8,128)(2,1)S(1)}, u32[]{:S(2)}, u32[]{:S(2)}) %collective-permute-start.4) | collective-permute-done | bytes 1048608 | tf_op jit(solution)/shard_map/ppermute | solution.py:211
  26.3 0.0 copy-start.4
  26.3 1.0 copy-done.4
  27.3 9.4 %all-to-all-done.1.got_ref = bf16[16,16,1152]{2,1,0:T(8,128)(2,1)S(1)} async-done(((bf16[16,16,1152]{2,1,0:T(8,128)(2,1)}), bf16[16,16,1152]{2,1,0:T(8,128)(2,1)S(1)}, u32[]{:S(2)}, u32[]{:S(2)}) %all-to-all-start.1) | async-done | bytes 589856 | tf_op jit(solution)/shard_map/all_to_all | solution.py:20
  36.7 0.0 copy-start.3
  36.7 1.2 %copy-done.3 = bf16[1,1024,512]{2,1,0:T(8,128)(2,1)S(1)} copy-done((bf16[1,1024,512]{2,1,0:T(8,128)(2,1)S(1)}, bf16[1,1024,512]{2,1,0:T(8,128)(2,1)}, u32[]{:S(2)}) %copy-start.3) | copy-done | bytes 1048600
  37.9 0.0 copy-start.5
  37.9 1.2 %copy-done.5 = bf16[1,512,1024]{2,1,0:T(8,128)(2,1)S(1)} copy-done((bf16[1,512,1024]{2,1,0:T(8,128)(2,1)S(1)}, bf16[1,512,1024]{2,1,0:T(8,128)(2,1)}, u32[]{:S(2)}) %copy-start.5) | copy-done | bytes 1048600
  39.2 1.1 shard_map.48
  40.2 7.2 %all_to_all.26 = bf16[4,16,1024]{2,1,0:T(8,128)(2,1)S(1)} all-to-all(bf16[4,16,1024]{2,1,0:T(8,128)(2,1)S(1)} %shard_map.48), channel_id=1, replica_groups=mesh['x'=4,'zla'=2,'zlb'=2,'c'=2,'zh'=4,'y'=4] {'zla','zlb'}, dimensions={0} | all-to-all | bytes 262144 | tf_op jit(solution)/shard_map/all_to_all | solution.py:20
  47.4 1.1 broadcast_in_dim.3
  48.5 4.8 %all-to-all-start.3 = ((bf16[16,32,1024]{2,1,0:T(8,128)(2,1)}), bf16[16,32,1024]{2,1,0:T(8,128)(2,1)S(1)}, u32[]{:S(2)}, u32[]{:S(2)}) async-start(bf16[16,32,1024]{2,1,0:T(8,128)(2,1)} %broadcast_in_dim.3), calls=%async_computation.3 | async-start | bytes 2097152 | tf_op jit(solution)/shard_map/all_to_all | solution.py:20
  53.4 0.3 shard_map.47
  53.6 3.3 %collective-permute-start = (bf16[272,128]{1,0:T(8,128)(2,1)S(1)}, bf16[272,128]{1,0:T(8,128)(2,1)S(1)}, u32[]{:S(2)}, u32[]{:S(2)}) collective-permute-start(bf16[272,128]{1,0:T(8,128)(2,1)S(1)} %get-tuple-element.13), channel_id=1, source_target_pairs={{0,1},{1,2},{2,3},{3,0},{4,5},{5,6},{6,7},{7,4},{8,9},{9,10},{10,1... | collective-permute-start | bytes 208904 | tf_op jit(solution)/shard_map/ppermute | solution.py:225
  56.9 4.3 %collective-permute-start.1 = (bf16[272,128]{1,0:T(8,128)(2,1)S(1)}, bf16[272,128]{1,0:T(8,128)(2,1)S(1)}, u32[]{:S(2)}, u32[]{:S(2)}) collective-permute-start(bf16[272,128]{1,0:T(8,128)(2,1)S(1)} %get-tuple-element.14), channel_id=1, source_target_pairs={{0,2},{1,3},{2,0},{3,1},{4,6},{5,7},{6,4},{7,5},{8,10},{9,11},{10,... | collective-permute-start | bytes 208904 | tf_op jit(solution)/shard_map/ppermute | solution.py:225
  61.2 3.1 %collective-permute-start.2 = (bf16[272,128]{1,0:T(8,128)(2,1)S(1)}, bf16[272,128]{1,0:T(8,128)(2,1)S(1)}, u32[]{:S(2)}, u32[]{:S(2)}) collective-permute-start(bf16[272,128]{1,0:T(8,128)(2,1)S(1)} %get-tuple-element.15), channel_id=1, source_target_pairs={{0,3},{1,0},{2,1},{3,2},{4,7},{5,4},{6,5},{7,6},{8,11},{9,8},{10,9... | collective-permute-start | bytes 208904 | tf_op jit(solution)/shard_map/ppermute | solution.py:225
  64.3 0.8 collective-permute-done.r1
  65.1 6.9 %collective-permute-done.1.r2 = bf16[272,128]{1,0:T(8,128)(2,1)S(1)} collective-permute-done((bf16[272,128]{1,0:T(8,128)(2,1)S(1)}, bf16[272,128]{1,0:T(8,128)(2,1)S(1)}, u32[]{:S(2)}, u32[]{:S(2)}) %collective-permute-start.1) | collective-permute-done | bytes 69664 | tf_op jit(solution)/shard_map/ppermute | solution.py:225
  72.1 0.0 collective-permute-done.2.r3
  72.1 0.0 all-to-all-done.3
  72.1 1.6 %shard_map.49 = bf16[8,264,128]{2,1,0:T(8,128)(2,1)} custom-call(s32[1]{0:T(128)} %bitcast.1.at_ref, bf16[272,128]{1,0:T(8,128)(2,1)S(1)} %get-tuple-element.12.r0, bf16[272,128]{1,0:T(8,128)(2,1)S(1)} %collective-permute-done.r1, bf16[272,128]{1,0:T(8,128)(2,1)S(1)} %collective-permute-done.1.r2, bf16[272,128]{1,0:T(8,128)(2,1)S(1)} %collective-permute-done.2.r3, ...), custom_call_target="tpu_custom_call" | custom-call | tf_op jit(solution)/shard_map/pallas_call | solution.py:173
  73.7 14.5 %all-to-all-start.4 = ((bf16[8,264,128]{2,1,0:T(8,128)(2,1)}), bf16[8,264,128]{2,1,0:T(8,128)(2,1)S(1)}, u32[]{:S(2)}, u32[]{:S(2)}) async-start(bf16[8,264,128]{2,1,0:T(8,128)(2,1)} %shard_map.49), calls=%async_computation.4 | async-start | bytes 1081344 | tf_op jit(solution)/shard_map/all_to_all | solution.py:20
  88.2 29.7 %all-to-all-done.4.got_ref = bf16[8,264,128]{2,1,0:T(8,128)(2,1)S(1)} async-done(((bf16[8,264,128]{2,1,0:T(8,128)(2,1)}), bf16[8,264,128]{2,1,0:T(8,128)(2,1)S(1)}, u32[]{:S(2)}, u32[]{:S(2)}) %all-to-all-start.4) | async-done | bytes 540704 | tf_op jit(solution)/shard_map/all_to_all | solution.py:20
  117.8 1.4 %shard_map.50 = bf16[2,32,1024]{2,1,0:T(8,128)(2,1)} custom-call(s32[1]{0:T(128)} %bitcast.at_ref, bf16[8,264,128]{2,1,0:T(8,128)(2,1)S(1)} %all-to-all-done.4.got_ref), custom_call_target="tpu_custom_call" | custom-call | tf_op jit(solution)/shard_map/pallas_call | solution.py:173
  (1 shorter events, 0.0 us)
Async XLA Ops:
  0.0 13.2 %copy-start.6 = (bf16[1024,128]{1,0:T(8,128)(2,1)S(1)}, bf16[1024,128]{1,0:T(8,128)(2,1)}, u32[]{:S(2)}) copy-start(bf16[1024,128]{1,0:T(8,128)(2,1)} %router_ref.1) | copy-start | bytes 786436
  13.2 6.2 %copy-start = (bf16[1,1024,512]{2,1,0:T(8,128)(2,1)S(1)}, bf16[1,1024,512]{2,1,0:T(8,128)(2,1)}, u32[]{:S(2)}) copy-start(bf16[1,1024,512]{2,1,0:T(8,128)(2,1)} %a_ref.1) | copy-start | bytes 3145732
  13.2 8.5 %copy-start.1 = (bf16[1,512,1024]{2,1,0:T(8,128)(2,1)S(1)}, bf16[1,512,1024]{2,1,0:T(8,128)(2,1)}, u32[]{:S(2)}) copy-start(bf16[1,512,1024]{2,1,0:T(8,128)(2,1)} %b_ref.1) | copy-start | bytes 3145732
  15.8 20.9 %all-to-all-start.1 = ((bf16[16,16,1152]{2,1,0:T(8,128)(2,1)}), bf16[16,16,1152]{2,1,0:T(8,128)(2,1)S(1)}, u32[]{:S(2)}, u32[]{:S(2)}) async-start(bf16[16,16,1152]{2,1,0:T(8,128)(2,1)} %get-tuple-element.16), calls=%async_computation.1 | async-start | bytes 1179648 | tf_op jit(solution)/shard_map/all_to_all | solution.py:20
  19.4 4.6 %collective-permute-start.3 = (bf16[1,1024,512]{2,1,0:T(8,128)(2,1)S(1)}, bf16[1,1024,512]{2,1,0:T(8,128)(2,1)S(1)}, u32[]{:S(2)}, u32[]{:S(2)}) collective-permute-start(bf16[1,1024,512]{2,1,0:T(8,128)(2,1)S(1)} %copy-done), channel_id=1, source_target_pairs={{0,16},{16,0},{1,17},{17,1},{2,18},{18,2},{3,19},{19,3},{4,20},{20... | collective-permute-start | bytes 3145736 | tf_op jit(solution)/shard_map/ppermute | solution.py:210
  21.7 4.6 %collective-permute-start.4 = (bf16[1,512,1024]{2,1,0:T(8,128)(2,1)S(1)}, bf16[1,512,1024]{2,1,0:T(8,128)(2,1)S(1)}, u32[]{:S(2)}, u32[]{:S(2)}) collective-permute-start(bf16[1,512,1024]{2,1,0:T(8,128)(2,1)S(1)} %copy-done.1), channel_id=1, source_target_pairs={{0,16},{16,0},{1,17},{17,1},{2,18},{18,2},{3,19},{19,3},{4,20},{20... | collective-permute-start | bytes 3145736 | tf_op jit(solution)/shard_map/ppermute | solution.py:211
  24.0 1.0 copy-start.2
  26.3 1.0 copy-start.4
  36.7 1.2 %copy-start.3 = (bf16[1,1024,512]{2,1,0:T(8,128)(2,1)S(1)}, bf16[1,1024,512]{2,1,0:T(8,128)(2,1)}, u32[]{:S(2)}) copy-start(bf16[1,1024,512]{2,1,0:T(8,128)(2,1)} %copy-done.2) | copy-start | bytes 3145732
  37.9 1.2 %copy-start.5 = (bf16[1,512,1024]{2,1,0:T(8,128)(2,1)S(1)}, bf16[1,512,1024]{2,1,0:T(8,128)(2,1)}, u32[]{:S(2)}) copy-start(bf16[1,512,1024]{2,1,0:T(8,128)(2,1)} %copy-done.4) | copy-start | bytes 3145732
  48.5 23.5 %all-to-all-start.3 = ((bf16[16,32,1024]{2,1,0:T(8,128)(2,1)}), bf16[16,32,1024]{2,1,0:T(8,128)(2,1)S(1)}, u32[]{:S(2)}, u32[]{:S(2)}) async-start(bf16[16,32,1024]{2,1,0:T(8,128)(2,1)} %broadcast_in_dim.3), calls=%async_computation.3 | async-start | bytes 2097152 | tf_op jit(solution)/shard_map/all_to_all | solution.py:20
  53.6 11.5 %collective-permute-start = (bf16[272,128]{1,0:T(8,128)(2,1)S(1)}, bf16[272,128]{1,0:T(8,128)(2,1)S(1)}, u32[]{:S(2)}, u32[]{:S(2)}) collective-permute-start(bf16[272,128]{1,0:T(8,128)(2,1)S(1)} %get-tuple-element.13), channel_id=1, source_target_pairs={{0,1},{1,2},{2,3},{3,0},{4,5},{5,6},{6,7},{7,4},{8,9},{9,10},{10,1... | collective-permute-start | bytes 208904 | tf_op jit(solution)/shard_map/ppermute | solution.py:225
  56.9 15.2 %collective-permute-start.1 = (bf16[272,128]{1,0:T(8,128)(2,1)S(1)}, bf16[272,128]{1,0:T(8,128)(2,1)S(1)}, u32[]{:S(2)}, u32[]{:S(2)}) collective-permute-start(bf16[272,128]{1,0:T(8,128)(2,1)S(1)} %get-tuple-element.14), channel_id=1, source_target_pairs={{0,2},{1,3},{2,0},{3,1},{4,6},{5,7},{6,4},{7,5},{8,10},{9,11},{10,... | collective-permute-start | bytes 208904 | tf_op jit(solution)/shard_map/ppermute | solution.py:225
  61.2 10.8 %collective-permute-start.2 = (bf16[272,128]{1,0:T(8,128)(2,1)S(1)}, bf16[272,128]{1,0:T(8,128)(2,1)S(1)}, u32[]{:S(2)}, u32[]{:S(2)}) collective-permute-start(bf16[272,128]{1,0:T(8,128)(2,1)S(1)} %get-tuple-element.15), channel_id=1, source_target_pairs={{0,3},{1,0},{2,1},{3,2},{4,7},{5,4},{6,5},{7,6},{8,11},{9,8},{10,9... | collective-permute-start | bytes 208904 | tf_op jit(solution)/shard_map/ppermute | solution.py:225
  73.7 44.1 %all-to-all-start.4 = ((bf16[8,264,128]{2,1,0:T(8,128)(2,1)}), bf16[8,264,128]{2,1,0:T(8,128)(2,1)S(1)}, u32[]{:S(2)}, u32[]{:S(2)}) async-start(bf16[8,264,128]{2,1,0:T(8,128)(2,1)} %shard_map.49), calls=%async_computation.4 | async-start | bytes 1081344 | tf_op jit(solution)/shard_map/all_to_all | solution.py:20

commit v3 on v2

--- a/solution.py
+++ b/solution.py
@@ -79,8 +79,9 @@
     for y in range(n):
         rows = []
         for c in range(cores):
-            at = [(c * n + z) * LANES + y * per for z in range(n)]
-            logits = jnp.concatenate([logit_ref[i : i + per] for i in at], axis=0).T
+            at = [(c * n + (at_ref[1] + j) % n) * LANES + y * per for j in range(n)]
+            at = [pl.multiple_of(i, per) for i in at]
+            logits = jnp.concatenate([logit_ref[pl.ds(i, per)] for i in at], axis=0).T
             top = logits.max(axis=0, keepdims=True)
             hold[y, c * slots : (c + 1) * slots] = jnp.exp(logits - top).astype(bf16)
             rows += in_three(top) + [zero] * 5
@@ -101,12 +102,24 @@
         out_ref[k] = out
 
 
-def mix_kernel(at_ref, r0, r1, r2, r3, found_ref, out_ref):
+def pair_kernel(got_ref, out_ref):
+    pairs = out_ref.shape[1] // SLOTS
+    each = got_ref.shape[0] // pairs
+    for p in range(pairs):
+        out = 0.0
+        for k in range(each):
+            out = out + got_ref[p * each + k].astype(f32)
+        out = out.astype(bf16)
+        for k in range(out_ref.shape[0]):
+            out_ref[k, p * SLOTS : (p + 1) * SLOTS] = out
+
+
+def mix_kernel(at_ref, r0, r1, r2, r3, found_ref, *outs):
     rs = (r0, r1, r2, r3)
     n, slots = len(rs), found_ref.shape[0] * found_ref.shape[2]
     width = found_ref.shape[-1]
     cores = r0.shape[0] // slots
-    nz = out_ref.shape[0] // cores
+    nz = len(outs)
     per = LANES // nz
     weights, stats = [[] for _ in rs], []
     for c in range(cores):
@@ -125,7 +138,7 @@
             weights[k].append((e2[k] * scale).T.astype(bf16))
         zero = jnp.zeros((2, LANES), f32)
         rows = jnp.concatenate(in_three(top) + in_three(total) + [zero], axis=0)
-        stats.append(rows.astype(bf16))
+        stats.append(rows)
     out = 0.0
     for k in range(n):
         y = (at_ref[0] + n - k) % n
@@ -134,24 +147,24 @@
     out = out.astype(bf16)
     for c in range(cores):
         for z in range(nz):
-            at, to = c * LANES + z * per, c * nz + z
+            at = c * LANES + z * per
             for j in range(width // LANES):
-                out_ref[to, j * per : (j + 1) * per] = out[at : at + per, j * LANES : (j + 1) * LANES]
-            out_ref[to, width // LANES * per :] = stats[c]
-
-
-def last_kernel(at_ref, got_ref, out_ref, hold):
-    seqs, per, width = out_ref.shape
-    n = got_ref.shape[0] // seqs
+                outs[z][c, j * per : (j + 1) * per] = out[at : at + per, j * LANES : (j + 1) * LANES]
+            outs[z][c, width // LANES * per :] = stats[c].astype(bf16)
+
+
+def last_kernel(at_ref, *refs):
+    gots, (keep_ref, give_ref, hold) = refs[:-3], refs[-3:]
+    cores, per, width = hold.shape
+    n = len(gots)
     end = width // LANES * per
-    both = [got_ref[k, end:].astype(f32) for k in range(seqs * n)]
+    both = [gots[k][c, end:].astype(f32) for c in range(cores) for k in range(n)]
     both = both + [jnp.zeros((LANES - 8 * len(both), LANES), f32)]
-    hold[...] = jnp.concatenate(both, axis=0).T
-    cols = hold[pl.ds(at_ref[0] * per, per)]
-    for s in range(seqs):
+    both = jnp.concatenate(both, axis=0).T
+    for c in range(cores):
         tops, totals = [], []
         for k in range(n):
-            i = 8 * (s * n + k)
+            i, cols = 8 * (c * n + k), both[k * per : (k + 1) * per]
             tops.append(cols[:, i : i + 1] + cols[:, i + 1 : i + 2] + cols[:, i + 2 : i + 3])
             totals.append(cols[:, i + 3 : i + 4] + cols[:, i + 4 : i + 5] + cols[:, i + 5 : i + 6])
         top = functools.reduce(jnp.maximum, tops)
@@ -161,11 +174,18 @@
         for j in range(width // LANES):
             out = 0.0
             for k in range(n):
-                out = out + got_ref[s * n + k, j * per : (j + 1) * per].astype(f32) * shares[k]
-            out_ref[s, :, j * LANES : (j + 1) * LANES] = out.astype(bf16)
-
-
-def call(kernel, outs, *args, scalar=False, scratch=()):
+                out = out + gots[k][c, j * per : (j + 1) * per].astype(f32) * shares[k]
+            hold[c, :, j * LANES : (j + 1) * LANES] = out.astype(bf16)
+    keep_ref[...] = hold[at_ref[2]]
+    give_ref[...] = hold[1 - at_ref[2]]
+
+
+def join_kernel(at_ref, keep_ref, got_ref, out_ref):
+    out_ref[at_ref[2]] = keep_ref[...]
+    out_ref[1 - at_ref[2]] = got_ref[1 - at_ref[2]]
+
+
+def call(kernel, outs, *args, scalar=False, scratch=(), mib=16):
     kind = pltpu.MemorySpace.VMEM
     specs = [pl.BlockSpec(memory_space=kind) for _ in args]
     if scalar:
@@ -176,7 +196,7 @@
         in_specs=specs,
         out_specs=jax.tree.map(lambda _: pl.BlockSpec(memory_space=kind), outs),
         scratch_shapes=scratch,
-        compiler_params=pltpu.CompilerParams(vmem_limit_bytes=40 << 20),
+        compiler_params=pltpu.CompilerParams(vmem_limit_bytes=mib << 20),
     )(*args)
 
 
@@ -191,8 +211,7 @@
     nx, nzla, nzlb, nc, nzh, ny = (lax.axis_size(a) for a in AXES)
     assert each == nzh * LANES and slots == nx * nzla * SLOTS
     assert nzh == ny == nx
-    here_y = lax.axis_index("y").astype(jnp.int32).reshape(1)
-    here_zh = lax.axis_index("zh").astype(jnp.int32).reshape(1)
+    here = jnp.stack([lax.axis_index(a).astype(jnp.int32) for a in ("y", "zh", "c")])
     per = LANES // nzh
 
     own = swap(tokens, "c")
@@ -214,7 +233,7 @@
     rows = call(
         row_kernel,
         (shape(block, LANES),) * ny,
-        here_y,
+        here,
         logits,
         scalar=True,
         scratch=(pltpu.VMEM((ny, block, LANES), bf16),),
@@ -227,25 +246,29 @@
     out = call(ffn_kernel, shape(nzla * nzlb, SLOTS, width), arrived, w_in, w_in2, w_out, w_out2)
 
     got = swap(out, ("zla", "zlb"))
-    got = got.reshape(nzla, nzlb, SLOTS, width).astype(f32).sum(axis=1).astype(bf16)
-    got = got.reshape(nzla * SLOTS, width)
-
-    found = swap(jnp.broadcast_to(got, (nx * ny, *got.shape)), ("x", "y"))
-    found = found.reshape(nx, ny, *got.shape)
+
+    got = call(pair_kernel, shape(nx * ny, nzla * SLOTS, width), got)
+
+    found = swap(got, ("x", "y")).reshape(nx, ny, nzla * SLOTS, width)
 
     block = width // LANES * per + 8
-    out = call(mix_kernel, shape(nc * nzh, block, LANES), here_y, *rows, found, scalar=True)
-
-    out = swap(out, ("c", "zh"))
-
-    return call(
+    outs = list(call(mix_kernel, (shape(nc, block, LANES),) * nzh, here, *rows, found, scalar=True))
+
+    for k in range(1, nzh):
+        outs[k] = lax.ppermute(outs[k], "zh", [(i, (i + k) % nzh) for i in range(nzh)])
+
+    keep, give = call(
         last_kernel,
-        shape(nc, per, width),
-        here_zh,
-        out,
+        (shape(per, width),) * 2,
+        here,
+        *outs,
         scalar=True,
-        scratch=(pltpu.VMEM((LANES, LANES), f32),),
-    )
+        scratch=(pltpu.VMEM((nc, per, width), bf16),),
+    )
+
+    got = lax.all_gather(give, "c")
+
+    return call(join_kernel, shape(nc, per, width), here, keep, got, scalar=True)
 
 
 def solution(mesh):

time: 120 us -> 121 us (level)
  waiting for transfers between devices: 48.4 us -> 38 us
  starting transfers between devices: 37.9 us -> 45.3 us
  Pallas kernels: 6.93 us -> 9.41 us
  blocking collectives: 20.4 us -> 22.5 us
    all_to_all x3 -> x2, waiting for transfers between devices: 39.1 us -> 9.47 us  [swap(): return lax.all_to_all(tiles, axis, split_axis=0, concat_axis=0, tiled=True)]
    ppermute x0 -> x3, starting transfers between devices: none -> 21.9 us  [shards(): lax.ppermute(outs[k], 'zh', [(i, (i + k) % nzh) for i in range(nzh)])]
    ppermute x0 -> x3, waiting for transfers between devices: none -> 19.8 us  [shards(): lax.ppermute(outs[k], 'zh', [(i, (i + k) % nzh) for i in range(nzh)])]
    all_to_all x3 -> x2, starting transfers between devices: 22.9 us -> 8.39 us  [swap(): return lax.all_to_all(tiles, axis, split_axis=0, concat_axis=0, tiled=True)]
    pallas_call x5 -> x7, Pallas kernels: 6.93 us -> 9.41 us  [call(): pl.pallas_call(kernel, out_shape=outs, in_specs=specs, out_specs=jax.tree...]
    all_gather x0 -> x1, blocking collectives: none -> 2.09 us  [shards(): got = lax.all_gather(give, 'c')]
  transfers between devices with their start and end apart: 8 -> 10, of which waited for: 6 -> 7; matrix products, arithmetic and copies ran while one was open for 0% -> 0% of each run, Pallas kernels for 0% -> 1%
where the time goes in v3:
time: 121 us; the launch traced here: 120 us
  starting transfers between devices  45.3 us (37%)
  waiting for transfers between devices  38 us (31%)
  blocking collectives  22.5 us (19%)
  Pallas kernels  9.41 us (8%)
  local copies, waits for them, and re-layouts  4.43 us (4%)
    ppermute x3, starting transfers between devices, shards(): lax.ppermute(outs[k], 'zh', [(i, (i + k) % nzh) for i in range(nzh)])  21.9 us
    all_to_all x2, blocking collectives, swap(): return lax.all_to_all(tiles, axis, split_axis=0, concat_axis=0, tiled=True)  20.4 us
    ppermute x3, waiting for transfers between devices, shards(): lax.ppermute(outs[k], 'zh', [(i, (i + k) % nzh) for i in range(nzh)])  19.8 us
    ppermute x3, starting transfers between devices, shards(): rows[k] = lax.ppermute(rows[k], 'y', [(i, (i + k) % ny) for i in range(ny)])  10.7 us
    all_to_all x2, waiting for transfers between devices, swap(): return lax.all_to_all(tiles, axis, split_axis=0, concat_axis=0, tiled=True)  9.47 us
    pallas_call x7, Pallas kernels, call(): pl.pallas_call(kernel, out_shape=outs, in_specs=specs, out_specs=jax.tree...  9.41 us
    all_to_all x2, starting transfers between devices, swap(): return lax.all_to_all(tiles, axis, split_axis=0, concat_axis=0, tiled=True)  8.39 us
    ppermute x3, waiting for transfers between devices, shards(): rows[k] = lax.ppermute(rows[k], 'y', [(i, (i + k) % ny) for i in range(ny)])  7.24 us
  transfers between devices with their start and end apart: 10, of which 7 were waited for; matrix products, arithmetic and copies ran while one was open for 0% of the time, Pallas kernels for 1%

profile of v3, /device:TPU:1, one launch (start us, length us, event | category | flops | bytes accessed | tf_op | source)
XLA Modules:
  0.0 119.9 jit_solution(9146161364224035146)
XLA Ops:
  0.0 0.0 copy-start.6
  0.0 13.2 %all_to_all.20.tok_ref = bf16[2,512,1024]{2,1,0:T(8,128)(2,1)S(1)} all-to-all(bf16[2,512,1024]{2,1,0:T(8,128)(2,1)} %param.4), channel_id=1, replica_groups=mesh['x'=4,'zla'=2,'zlb'=2,'c'=2,'zh'=4,'y'=4] {'c'}, dimensions={0} | all-to-all | bytes 4194304 | tf_op jit(solution)/shard_map/all_to_all | solution.py:20
  13.2 0.0 copy-done.6
  13.2 0.0 copy-start
  13.2 0.0 copy-start.1
  13.2 2.6 %shard_map.46 = (bf16[16,16,1152]{2,1,0:T(8,128)(2,1)}, f32[1024,128]{1,0:T(8,128)S(1)}) custom-call(bf16[2,512,1024]{2,1,0:T(8,128)(2,1)S(1)} %all_to_all.20.tok_ref, bf16[1024,128]{1,0:T(8,128)(2,1)S(1)} %copy-done.6), custom_call_target="tpu_custom_call" | custom-call | tf_op jit(solution)/shard_map/pallas_call | solution.py:193
  15.8 3.6 %all-to-all-start.1 = ((bf16[16,16,1152]{2,1,0:T(8,128)(2,1)}), bf16[16,16,1152]{2,1,0:T(8,128)(2,1)S(1)}, u32[]{:S(2)}, u32[]{:S(2)}) async-start(bf16[16,16,1152]{2,1,0:T(8,128)(2,1)} %get-tuple-element.22), calls=%async_computation.1 | async-start | bytes 1179648 | tf_op jit(solution)/shard_map/all_to_all | solution.py:20
  19.4 0.0 copy-done
  19.4 2.3 %collective-permute-start.3 = (bf16[1,1024,512]{2,1,0:T(8,128)(2,1)S(1)}, bf16[1,1024,512]{2,1,0:T(8,128)(2,1)S(1)}, u32[]{:S(2)}, u32[]{:S(2)}) collective-permute-start(bf16[1,1024,512]{2,1,0:T(8,128)(2,1)S(1)} %copy-done), channel_id=1, source_target_pairs={{0,16},{16,0},{1,17},{17,1},{2,18},{18,2},{3,19},{19,3},{4,20},{20... | collective-permute-start | bytes 3145736 | tf_op jit(solution)/shard_map/ppermute | solution.py:229
  21.7 0.0 copy-done.1
  21.7 2.0 %collective-permute-start.4 = (bf16[1,512,1024]{2,1,0:T(8,128)(2,1)S(1)}, bf16[1,512,1024]{2,1,0:T(8,128)(2,1)S(1)}, u32[]{:S(2)}, u32[]{:S(2)}) collective-permute-start(bf16[1,512,1024]{2,1,0:T(8,128)(2,1)S(1)} %copy-done.1), channel_id=1, source_target_pairs={{0,16},{16,0},{1,17},{17,1},{2,18},{18,2},{3,19},{19,3},{4,20},{20... | collective-permute-start | bytes 3145736 | tf_op jit(solution)/shard_map/ppermute | solution.py:230
  23.8 0.2 collective-permute-done.3.a2_ref
  24.0 0.0 copy-start.2
  24.0 1.0 copy-done.2
  25.0 1.3 %collective-permute-done.4.b2_ref = bf16[1,512,1024]{2,1,0:T(8,128)(2,1)S(1)} collective-permute-done((bf16[1,512,1024]{2,1,0:T(8,128)(2,1)S(1)}, bf16[1,512,1024]{2,1,0:T(8,128)(2,1)S(1)}, u32[]{:S(2)}, u32[]{:S(2)}) %collective-permute-start.4) | collective-permute-done | bytes 1048608 | tf_op jit(solution)/shard_map/ppermute | solution.py:230
  26.3 0.0 copy-start.4
  26.3 1.0 copy-done.4
  27.2 9.5 %all-to-all-done.1.got_ref = bf16[16,16,1152]{2,1,0:T(8,128)(2,1)S(1)} async-done(((bf16[16,16,1152]{2,1,0:T(8,128)(2,1)}), bf16[16,16,1152]{2,1,0:T(8,128)(2,1)S(1)}, u32[]{:S(2)}, u32[]{:S(2)}) %all-to-all-start.1) | async-done | bytes 589856 | tf_op jit(solution)/shard_map/all_to_all | solution.py:20
  36.7 0.0 copy-start.3
  36.7 1.2 %copy-done.3 = bf16[1,1024,512]{2,1,0:T(8,128)(2,1)S(1)} copy-done((bf16[1,1024,512]{2,1,0:T(8,128)(2,1)S(1)}, bf16[1,1024,512]{2,1,0:T(8,128)(2,1)}, u32[]{:S(2)}) %copy-start.3) | copy-done | bytes 1048600
  37.9 0.0 copy-start.5
  37.9 1.2 %copy-done.5 = bf16[1,512,1024]{2,1,0:T(8,128)(2,1)S(1)} copy-done((bf16[1,512,1024]{2,1,0:T(8,128)(2,1)S(1)}, bf16[1,512,1024]{2,1,0:T(8,128)(2,1)}, u32[]{:S(2)}) %copy-start.5) | copy-done | bytes 1048600
  39.2 1.1 shard_map.48
  40.2 7.2 %all_to_all.21.got_ref = bf16[4,16,1024]{2,1,0:T(8,128)(2,1)S(1)} all-to-all(bf16[4,16,1024]{2,1,0:T(8,128)(2,1)S(1)} %shard_map.48), channel_id=1, replica_groups=mesh['x'=4,'zla'=2,'zlb'=2,'c'=2,'zh'=4,'y'=4] {'zla','zlb'}, dimensions={0} | all-to-all | bytes 262144 | tf_op jit(solution)/shard_map/all_to_all | solution.py:20
  47.4 1.1 shard_map.49
  48.5 4.8 %all-to-all-start.3 = ((bf16[16,32,1024]{2,1,0:T(8,128)(2,1)}), bf16[16,32,1024]{2,1,0:T(8,128)(2,1)S(1)}, u32[]{:S(2)}, u32[]{:S(2)}) async-start(bf16[16,32,1024]{2,1,0:T(8,128)(2,1)} %shard_map.49), calls=%async_computation.3 | async-start | bytes 2097152 | tf_op jit(solution)/shard_map/all_to_all | solution.py:20
  53.3 0.1 pad_add_fusion.at_ref
  53.4 0.8 shard_map.47
  54.2 3.3 %collective-permute-start = (bf16[272,128]{1,0:T(8,128)(2,1)S(1)}, bf16[272,128]{1,0:T(8,128)(2,1)S(1)}, u32[]{:S(2)}, u32[]{:S(2)}) collective-permute-start(bf16[272,128]{1,0:T(8,128)(2,1)S(1)} %get-tuple-element.19), channel_id=1, source_target_pairs={{0,1},{1,2},{2,3},{3,0},{4,5},{5,6},{6,7},{7,4},{8,9},{9,10},{10,1... | collective-permute-start | bytes 208904 | tf_op jit(solution)/shard_map/ppermute | solution.py:244
  57.5 4.3 %collective-permute-start.1 = (bf16[272,128]{1,0:T(8,128)(2,1)S(1)}, bf16[272,128]{1,0:T(8,128)(2,1)S(1)}, u32[]{:S(2)}, u32[]{:S(2)}) collective-permute-start(bf16[272,128]{1,0:T(8,128)(2,1)S(1)} %get-tuple-element.20), channel_id=1, source_target_pairs={{0,2},{1,3},{2,0},{3,1},{4,6},{5,7},{6,4},{7,5},{8,10},{9,11},{10,... | collective-permute-start | bytes 208904 | tf_op jit(solution)/shard_map/ppermute | solution.py:244
  61.8 3.1 %collective-permute-start.2 = (bf16[272,128]{1,0:T(8,128)(2,1)S(1)}, bf16[272,128]{1,0:T(8,128)(2,1)S(1)}, u32[]{:S(2)}, u32[]{:S(2)}) collective-permute-start(bf16[272,128]{1,0:T(8,128)(2,1)S(1)} %get-tuple-element.21), channel_id=1, source_target_pairs={{0,3},{1,0},{2,1},{3,2},{4,7},{5,4},{6,5},{7,6},{8,11},{9,8},{10,9... | collective-permute-start | bytes 208904 | tf_op jit(solution)/shard_map/ppermute | solution.py:244
  64.9 5.5 %collective-permute-done.r1 = bf16[272,128]{1,0:T(8,128)(2,1)S(1)} collective-permute-done((bf16[272,128]{1,0:T(8,128)(2,1)S(1)}, bf16[272,128]{1,0:T(8,128)(2,1)S(1)}, u32[]{:S(2)}, u32[]{:S(2)}) %collective-permute-start) | collective-permute-done | bytes 69664 | tf_op jit(solution)/shard_map/ppermute | solution.py:244
  70.4 1.7 %collective-permute-done.1.r2 = bf16[272,128]{1,0:T(8,128)(2,1)S(1)} collective-permute-done((bf16[272,128]{1,0:T(8,128)(2,1)S(1)}, bf16[272,128]{1,0:T(8,128)(2,1)S(1)}, u32[]{:S(2)}, u32[]{:S(2)}) %collective-permute-start.1) | collective-permute-done | bytes 69664 | tf_op jit(solution)/shard_map/ppermute | solution.py:244
  72.2 0.0 collective-permute-done.2.r3
  72.2 0.0 all-to-all-done.3
  72.2 1.4 %shard_map.50 = (bf16[2,264,128]{2,1,0:T(8,128)(2,1)S(1)}, bf16[2,264,128]{2,1,0:T(8,128)(2,1)S(1)}, bf16[2,264,128]{2,1,0:T(8,128)(2,1)S(1)}, bf16[2,264,128]{2,1,0:T(8,128)(2,1)S(1)}) custom-call(s32[3]{0:T(128)S(1)} %pad_add_fusion.at_ref, bf16[272,128]{1,0:T(8,128)(2,1)S(1)} %get-tuple-element.18.r0, bf16[272,128]{1,0:T(8,128)(2,1)S(1)} %collective-permute-done.r1, ...), custom_call_target="tpu_custom_call" | custom-call | tf_op jit(solution)/shard_map/pallas_call | solution.py:193
  73.5 8.8 %collective-permute-start.5 = (bf16[2,264,128]{2,1,0:T(8,128)(2,1)S(1)}, bf16[2,264,128]{2,1,0:T(8,128)(2,1)S(1)}, u32[]{:S(2)}, u32[]{:S(2)}) collective-permute-start(bf16[2,264,128]{2,1,0:T(8,128)(2,1)S(1)} %get-tuple-element.24), channel_id=1, source_target_pairs={{0,4},{4,8},{8,12},{12,0},{1,5},{5,9},{9,13},{13,1},{2,6},{6,10},{... | collective-permute-start | bytes 405512 | tf_op jit(solution)/shard_map/ppermute | solution.py:258
  82.4 7.9 %collective-permute-start.6 = (bf16[2,264,128]{2,1,0:T(8,128)(2,1)S(1)}, bf16[2,264,128]{2,1,0:T(8,128)(2,1)S(1)}, u32[]{:S(2)}, u32[]{:S(2)}) collective-permute-start(bf16[2,264,128]{2,1,0:T(8,128)(2,1)S(1)} %get-tuple-element.25), channel_id=1, source_target_pairs={{0,8},{4,12},{8,0},{12,4},{1,9},{5,13},{9,1},{13,5},{2,10},{6,14},... | collective-permute-start | bytes 405512 | tf_op jit(solution)/shard_map/ppermute | solution.py:258
  90.3 5.2 %collective-permute-start.7 = (bf16[2,264,128]{2,1,0:T(8,128)(2,1)S(1)}, bf16[2,264,128]{2,1,0:T(8,128)(2,1)S(1)}, u32[]{:S(2)}, u32[]{:S(2)}) collective-permute-start(bf16[2,264,128]{2,1,0:T(8,128)(2,1)S(1)} %get-tuple-element.26), channel_id=1, source_target_pairs={{0,12},{4,0},{8,4},{12,8},{1,13},{5,1},{9,5},{13,9},{2,14},{6,2},{... | collective-permute-start | bytes 405512 | tf_op jit(solution)/shard_map/ppermute | solution.py:258
  95.5 0.0 collective-permute-done.5.refs_1_
  95.5 8.0 %collective-permute-done.6.refs_2_ = bf16[2,264,128]{2,1,0:T(8,128)(2,1)S(1)} collective-permute-done((bf16[2,264,128]{2,1,0:T(8,128)(2,1)S(1)}, bf16[2,264,128]{2,1,0:T(8,128)(2,1)S(1)}, u32[]{:S(2)}, u32[]{:S(2)}) %collective-permute-start.6) | collective-permute-done | bytes 135200 | tf_op jit(solution)/shard_map/ppermute | solution.py:258
  103.5 11.8 %collective-permute-done.7.refs_3_ = bf16[2,264,128]{2,1,0:T(8,128)(2,1)S(1)} collective-permute-done((bf16[2,264,128]{2,1,0:T(8,128)(2,1)S(1)}, bf16[2,264,128]{2,1,0:T(8,128)(2,1)S(1)}, u32[]{:S(2)}, u32[]{:S(2)}) %collective-permute-start.7) | collective-permute-done | bytes 135200 | tf_op jit(solution)/shard_map/ppermute | solution.py:258
  115.3 1.2 %shard_map.51 = (bf16[32,1024]{1,0:T(8,128)(2,1)S(1)}, bf16[32,1024]{1,0:T(8,128)(2,1)S(1)}) custom-call(s32[3]{0:T(128)S(1)} %pad_add_fusion.at_ref, bf16[2,264,128]{2,1,0:T(8,128)(2,1)S(1)} %get-tuple-element.23.refs_0_, bf16[2,264,128]{2,1,0:T(8,128)(2,1)S(1)} %collective-permute-done.5.refs_1_, bf16[2,264,128]{2,1,0:T(8,128)(2,1)S(1)} %collective-permute-done.6.refs_2_, ...), custom_call_target="tpu_custom_call" | custom-call | tf_op jit(solution)/shard_map/pallas_call | solution.py:193
  116.6 2.1 %all-gather = bf16[64,1024]{1,0:T(8,128)(2,1)S(1)} all-gather(bf16[32,1024]{1,0:T(8,128)(2,1)S(1)} %get-tuple-element.28), channel_id=2, replica_groups=mesh['x'=4,'zla'=2,'zlb'=2,'c'=2,'zh'=4,'y'=4] {'c'}, dimensions={0}, use_global_device_ids=true | all-gather | bytes 196608 | tf_op jit(solution)/shard_map/all_gather | solution.py:269
  118.7 1.2 %shard_map.52 = bf16[2,32,1024]{2,1,0:T(8,128)(2,1)} custom-call(s32[3]{0:T(128)S(1)} %pad_add_fusion.at_ref, bf16[32,1024]{1,0:T(8,128)(2,1)S(1)} %get-tuple-element.27.keep_ref, bf16[2,32,1024]{2,1,0:T(8,128)(2,1)S(1)} %bitcast.6), custom_call_target="tpu_custom_call" | custom-call | tf_op jit(solution)/shard_map/pallas_call | solution.py:193
Async XLA Ops:
  0.0 13.2 %copy-start.6 = (bf16[1024,128]{1,0:T(8,128)(2,1)S(1)}, bf16[1024,128]{1,0:T(8,128)(2,1)}, u32[]{:S(2)}) copy-start(bf16[1024,128]{1,0:T(8,128)(2,1)} %router_ref.1) | copy-start | bytes 786436
  13.2 6.2 %copy-start = (bf16[1,1024,512]{2,1,0:T(8,128)(2,1)S(1)}, bf16[1,1024,512]{2,1,0:T(8,128)(2,1)}, u32[]{:S(2)}) copy-start(bf16[1,1024,512]{2,1,0:T(8,128)(2,1)} %a_ref.1) | copy-start | bytes 3145732
  13.2 8.5 %copy-start.1 = (bf16[1,512,1024]{2,1,0:T(8,128)(2,1)S(1)}, bf16[1,512,1024]{2,1,0:T(8,128)(2,1)}, u32[]{:S(2)}) copy-start(bf16[1,512,1024]{2,1,0:T(8,128)(2,1)} %b_ref.1) | copy-start | bytes 3145732
  15.8 20.9 %all-to-all-start.1 = ((bf16[16,16,1152]{2,1,0:T(8,128)(2,1)}), bf16[16,16,1152]{2,1,0:T(8,128)(2,1)S(1)}, u32[]{:S(2)}, u32[]{:S(2)}) async-start(bf16[16,16,1152]{2,1,0:T(8,128)(2,1)} %get-tuple-element.22), calls=%async_computation.1 | async-start | bytes 1179648 | tf_op jit(solution)/shard_map/all_to_all | solution.py:20
  19.4 4.6 %collective-permute-start.3 = (bf16[1,1024,512]{2,1,0:T(8,128)(2,1)S(1)}, bf16[1,1024,512]{2,1,0:T(8,128)(2,1)S(1)}, u32[]{:S(2)}, u32[]{:S(2)}) collective-permute-start(bf16[1,1024,512]{2,1,0:T(8,128)(2,1)S(1)} %copy-done), channel_id=1, source_target_pairs={{0,16},{16,0},{1,17},{17,1},{2,18},{18,2},{3,19},{19,3},{4,20},{20... | collective-permute-start | bytes 3145736 | tf_op jit(solution)/shard_map/ppermute | solution.py:229
  21.7 4.6 %collective-permute-start.4 = (bf16[1,512,1024]{2,1,0:T(8,128)(2,1)S(1)}, bf16[1,512,1024]{2,1,0:T(8,128)(2,1)S(1)}, u32[]{:S(2)}, u32[]{:S(2)}) collective-permute-start(bf16[1,512,1024]{2,1,0:T(8,128)(2,1)S(1)} %copy-done.1), channel_id=1, source_target_pairs={{0,16},{16,0},{1,17},{17,1},{2,18},{18,2},{3,19},{19,3},{4,20},{20... | collective-permute-start | bytes 3145736 | tf_op jit(solution)/shard_map/ppermute | solution.py:230
  24.0 1.0 copy-start.2
  26.3 1.0 copy-start.4
  36.7 1.2 %copy-start.3 = (bf16[1,1024,512]{2,1,0:T(8,128)(2,1)S(1)}, bf16[1,1024,512]{2,1,0:T(8,128)(2,1)}, u32[]{:S(2)}) copy-start(bf16[1,1024,512]{2,1,0:T(8,128)(2,1)} %copy-done.2) | copy-start | bytes 3145732
  37.9 1.2 %copy-start.5 = (bf16[1,512,1024]{2,1,0:T(8,128)(2,1)S(1)}, bf16[1,512,1024]{2,1,0:T(8,128)(2,1)}, u32[]{:S(2)}) copy-start(bf16[1,512,1024]{2,1,0:T(8,128)(2,1)} %copy-done.4) | copy-start | bytes 3145732
  48.5 23.6 %all-to-all-start.3 = ((bf16[16,32,1024]{2,1,0:T(8,128)(2,1)}), bf16[16,32,1024]{2,1,0:T(8,128)(2,1)S(1)}, u32[]{:S(2)}, u32[]{:S(2)}) async-start(bf16[16,32,1024]{2,1,0:T(8,128)(2,1)} %shard_map.49), calls=%async_computation.3 | async-start | bytes 2097152 | tf_op jit(solution)/shard_map/all_to_all | solution.py:20
  54.2 16.2 %collective-permute-start = (bf16[272,128]{1,0:T(8,128)(2,1)S(1)}, bf16[272,128]{1,0:T(8,128)(2,1)S(1)}, u32[]{:S(2)}, u32[]{:S(2)}) collective-permute-start(bf16[272,128]{1,0:T(8,128)(2,1)S(1)} %get-tuple-element.19), channel_id=1, source_target_pairs={{0,1},{1,2},{2,3},{3,0},{4,5},{5,6},{6,7},{7,4},{8,9},{9,10},{10,1... | collective-permute-start | bytes 208904 | tf_op jit(solution)/shard_map/ppermute | solution.py:244
  57.5 14.7 %collective-permute-start.1 = (bf16[272,128]{1,0:T(8,128)(2,1)S(1)}, bf16[272,128]{1,0:T(8,128)(2,1)S(1)}, u32[]{:S(2)}, u32[]{:S(2)}) collective-permute-start(bf16[272,128]{1,0:T(8,128)(2,1)S(1)} %get-tuple-element.20), channel_id=1, source_target_pairs={{0,2},{1,3},{2,0},{3,1},{4,6},{5,7},{6,4},{7,5},{8,10},{9,11},{10,... | collective-permute-start | bytes 208904 | tf_op jit(solution)/shard_map/ppermute | solution.py:244
  61.8 10.3 %collective-permute-start.2 = (bf16[272,128]{1,0:T(8,128)(2,1)S(1)}, bf16[272,128]{1,0:T(8,128)(2,1)S(1)}, u32[]{:S(2)}, u32[]{:S(2)}) collective-permute-start(bf16[272,128]{1,0:T(8,128)(2,1)S(1)} %get-tuple-element.21), channel_id=1, source_target_pairs={{0,3},{1,0},{2,1},{3,2},{4,7},{5,4},{6,5},{7,6},{8,11},{9,8},{10,9... | collective-permute-start | bytes 208904 | tf_op jit(solution)/shard_map/ppermute | solution.py:244
  73.5 22.0 %collective-permute-start.5 = (bf16[2,264,128]{2,1,0:T(8,128)(2,1)S(1)}, bf16[2,264,128]{2,1,0:T(8,128)(2,1)S(1)}, u32[]{:S(2)}, u32[]{:S(2)}) collective-permute-start(bf16[2,264,128]{2,1,0:T(8,128)(2,1)S(1)} %get-tuple-element.24), channel_id=1, source_target_pairs={{0,4},{4,8},{8,12},{12,0},{1,5},{5,9},{9,13},{13,1},{2,6},{6,10},{... | collective-permute-start | bytes 405512 | tf_op jit(solution)/shard_map/ppermute | solution.py:258
  82.4 21.2 %collective-permute-start.6 = (bf16[2,264,128]{2,1,0:T(8,128)(2,1)S(1)}, bf16[2,264,128]{2,1,0:T(8,128)(2,1)S(1)}, u32[]{:S(2)}, u32[]{:S(2)}) collective-permute-start(bf16[2,264,128]{2,1,0:T(8,128)(2,1)S(1)} %get-tuple-element.25), channel_id=1, source_target_pairs={{0,8},{4,12},{8,0},{12,4},{1,9},{5,13},{9,1},{13,5},{2,10},{6,14},... | collective-permute-start | bytes 405512 | tf_op jit(solution)/shard_map/ppermute | solution.py:258
  90.3 25.0 %collective-permute-start.7 = (bf16[2,264,128]{2,1,0:T(8,128)(2,1)S(1)}, bf16[2,264,128]{2,1,0:T(8,128)(2,1)S(1)}, u32[]{:S(2)}, u32[]{:S(2)}) collective-permute-start(bf16[2,264,128]{2,1,0:T(8,128)(2,1)S(1)} %get-tuple-element.26), channel_id=1, source_target_pairs={{0,12},{4,0},{8,4},{12,8},{1,13},{5,1},{9,5},{13,9},{2,14},{6,2},{... | collective-permute-start | bytes 405512 | tf_op jit(solution)/shard_map/ppermute | solution.py:258

commit v4 on v3

--- a/solution.py
+++ b/solution.py
@@ -79,7 +79,7 @@
     for y in range(n):
         rows = []
         for c in range(cores):
-            at = [(c * n + (at_ref[1] + j) % n) * LANES + y * per for j in range(n)]
+            at = [((at_ref[2] ^ c) * n + (at_ref[1] ^ j)) * LANES + y * per for j in range(n)]
             at = [pl.multiple_of(i, per) for i in at]
             logits = jnp.concatenate([logit_ref[pl.ds(i, per)] for i in at], axis=0).T
             top = logits.max(axis=0, keepdims=True)
@@ -87,17 +87,27 @@
             rows += in_three(top) + [zero] * 5
         hold[y, cores * slots :] = jnp.concatenate(rows, axis=0).astype(bf16)
     for k in range(n):
-        outs[k][...] = hold[(at_ref[0] + k) % n]
-
-
-def ffn_kernel(got_ref, a_ref, a2_ref, b_ref, b2_ref, out_ref):
+        outs[k][...] = hold[at_ref[0] ^ k]
+
+
+def ffn_kernel(got_ref, a_ref, b_ref, a2_hbm, b2_hbm, out_ref, a2_ref, b2_ref, sem):
+    copies = (
+        pltpu.make_async_copy(a2_hbm, a2_ref, sem.at[0]),
+        pltpu.make_async_copy(b2_hbm, b2_ref, sem.at[1]),
+    )
+    for copy in copies:
+        copy.start()
     rows = blend(got_ref, [(k,) for k in range(got_ref.shape[0])]).astype(bf16)
-    out = 0.0
-    for a, b in ((a_ref, b_ref), (a2_ref, b2_ref)):
+
+    def part(a, b):
         hidden = jnp.dot(rows, a[0], preferred_element_type=f32)
         hidden = jax.nn.gelu(hidden, approximate=True).astype(bf16)
-        out = out + jnp.dot(hidden, b[0], preferred_element_type=f32)
-    out = out.astype(bf16)
+        return jnp.dot(hidden, b[0], preferred_element_type=f32)
+
+    out = part(a_ref, b_ref)
+    for copy in copies:
+        copy.wait()
+    out = (out + part(a2_ref, b2_ref)).astype(bf16)
     for k in range(out_ref.shape[0]):
         out_ref[k] = out
 
@@ -141,7 +151,7 @@
         stats.append(rows)
     out = 0.0
     for k in range(n):
-        y = (at_ref[0] + n - k) % n
+        y = at_ref[0] ^ k
         block = found_ref[:, y].reshape(slots, width)
         out = out + jnp.dot(jnp.concatenate(weights[k], axis=0), block, preferred_element_type=f32)
     out = out.astype(bf16)
@@ -153,9 +163,9 @@
             outs[z][c, width // LANES * per :] = stats[c].astype(bf16)
 
 
-def last_kernel(at_ref, *refs):
-    gots, (keep_ref, give_ref, hold) = refs[:-3], refs[-3:]
-    cores, per, width = hold.shape
+def last_kernel(*refs):
+    gots, outs = refs[:-2], refs[-2:]
+    cores, (per, width) = len(outs), outs[0].shape
     n = len(gots)
     end = width // LANES * per
     both = [gots[k][c, end:].astype(f32) for c in range(cores) for k in range(n)]
@@ -175,9 +185,7 @@
             out = 0.0
             for k in range(n):
                 out = out + gots[k][c, j * per : (j + 1) * per].astype(f32) * shares[k]
-            hold[c, :, j * LANES : (j + 1) * LANES] = out.astype(bf16)
-    keep_ref[...] = hold[at_ref[2]]
-    give_ref[...] = hold[1 - at_ref[2]]
+            outs[c][:, j * LANES : (j + 1) * LANES] = out.astype(bf16)
 
 
 def join_kernel(at_ref, keep_ref, got_ref, out_ref):
@@ -185,9 +193,11 @@
     out_ref[1 - at_ref[2]] = got_ref[1 - at_ref[2]]
 
 
-def call(kernel, outs, *args, scalar=False, scratch=(), mib=16):
+def call(kernel, outs, *args, scalar=False, scratch=(), far=0, mib=16):
     kind = pltpu.MemorySpace.VMEM
     specs = [pl.BlockSpec(memory_space=kind) for _ in args]
+    for k in range(far):
+        specs[-1 - k] = pl.BlockSpec(memory_space=pl.ANY)
     if scalar:
         specs[0] = pl.BlockSpec(memory_space=pltpu.MemorySpace.SMEM)
     return pl.pallas_call(
@@ -241,13 +251,29 @@
 
     rows = list(rows)
     for k in range(1, ny):
-        rows[k] = lax.ppermute(rows[k], "y", [(i, (i + k) % ny) for i in range(ny)])
-
-    out = call(ffn_kernel, shape(nzla * nzlb, SLOTS, width), arrived, w_in, w_in2, w_out, w_out2)
+        rows[k] = lax.ppermute(rows[k], "y", [(i, i ^ k) for i in range(ny)])
+
+    out = call(
+        ffn_kernel,
+        shape(nzla * nzlb, SLOTS, width),
+        arrived,
+        w_in,
+        w_out,
+        w_in2,
+        w_out2,
+        far=2,
+        scratch=(
+            pltpu.VMEM(w_in.shape, bf16),
+            pltpu.VMEM(w_out.shape, bf16),
+            pltpu.SemaphoreType.DMA((2,)),
+        ),
+    )
 
     got = swap(out, ("zla", "zlb"))
 
     got = call(pair_kernel, shape(nx * ny, nzla * SLOTS, width), got)
+
+    got, *rows = lax.optimization_barrier((got, *rows))
 
     found = swap(got, ("x", "y")).reshape(nx, ny, nzla * SLOTS, width)
 
@@ -255,16 +281,9 @@
     outs = list(call(mix_kernel, (shape(nc, block, LANES),) * nzh, here, *rows, found, scalar=True))
 
     for k in range(1, nzh):
-        outs[k] = lax.ppermute(outs[k], "zh", [(i, (i + k) % nzh) for i in range(nzh)])
-
-    keep, give = call(
-        last_kernel,
-        (shape(per, width),) * 2,
-        here,
-        *outs,
-        scalar=True,
-        scratch=(pltpu.VMEM((nc, per, width), bf16),),
-    )
+        outs[k] = lax.ppermute(outs[k], "zh", [(i, i ^ k) for i in range(nzh)])
+
+    keep, give = call(last_kernel, (shape(per, width),) * nc, *outs)
 
     got = lax.all_gather(give, "c")
 

time: 121 us -> 122 us (level)
  blocking collectives: 22.5 us -> 33.6 us
  starting transfers between devices: 45.3 us -> 39.5 us
  waiting for transfers between devices: 38 us -> 34.9 us
    all_to_all x2, blocking collectives: 20.4 us -> 29.3 us  [swap(): return lax.all_to_all(tiles, axis, split_axis=0, concat_axis=0, tiled=True)]
    ppermute x6, starting transfers between devices: 32.6 us -> 28.3 us  [the longest x3 18.7 us: shards(): outs[k] = lax.ppermute(outs[k], 'zh', [(i, i ^ k) for i in range(nzh)])]
    ppermute x6, waiting for transfers between devices: 27.1 us -> 23.9 us  [the longest x3 20.5 us: shards(): outs[k] = lax.ppermute(outs[k], 'zh', [(i, i ^ k) for i in range(nzh)])]
    all_gather x1, blocking collectives: 2.09 us -> 4.27 us  [shards(): got = lax.all_gather(give, 'c')]
    all_to_all x2, starting transfers between devices: 8.39 us -> 6.92 us  [swap(): return lax.all_to_all(tiles, axis, split_axis=0, concat_axis=0, tiled=True)]
where the time goes in v4:
time: 122 us; the launch traced here: 121 us
  starting transfers between devices  39.5 us (32%)
  waiting for transfers between devices  34.9 us (29%)
  blocking collectives  33.6 us (28%)
  Pallas kernels  8.79 us (7%)
  local copies, waits for them, and re-layouts  4.43 us (4%)
    all_to_all x2, blocking collectives, swap(): return lax.all_to_all(tiles, axis, split_axis=0, concat_axis=0, tiled=True)  29.3 us
    ppermute x3, waiting for transfers between devices, shards(): outs[k] = lax.ppermute(outs[k], 'zh', [(i, i ^ k) for i in range(nzh)])  20.5 us
    ppermute x3, starting transfers between devices, shards(): outs[k] = lax.ppermute(outs[k], 'zh', [(i, i ^ k) for i in range(nzh)])  18.7 us
    ppermute x3, starting transfers between devices, shards(): rows[k] = lax.ppermute(rows[k], 'y', [(i, i ^ k) for i in range(ny)])  9.58 us
    all_to_all x2, waiting for transfers between devices, swap(): return lax.all_to_all(tiles, axis, split_axis=0, concat_axis=0, tiled=True)  9.47 us
    pallas_call x7, Pallas kernels, call(): pl.pallas_call(kernel, out_shape=outs, in_specs=specs, out_specs=jax.tree...  8.79 us
    all_to_all x2, starting transfers between devices, swap(): return lax.all_to_all(tiles, axis, split_axis=0, concat_axis=0, tiled=True)  6.92 us
    unnamed x14, local copies, waits for them, and re-layouts  4.43 us
  transfers between devices with their start and end apart: 10, of which 7 were waited for; matrix products, arithmetic and copies ran while one was open for 0% of the time, Pallas kernels for 1%

profile of v4, /device:TPU:1, one launch (start us, length us, event | category | flops | bytes accessed | tf_op | source)
XLA Modules:
  0.0 121.4 jit_solution(15498219691985395292)
XLA Ops:
  0.0 0.0 copy-start.6
  0.0 13.2 %all_to_all.20.tok_ref = bf16[2,512,1024]{2,1,0:T(8,128)(2,1)S(1)} all-to-all(bf16[2,512,1024]{2,1,0:T(8,128)(2,1)} %param.4), channel_id=1, replica_groups=mesh['x'=4,'zla'=2,'zlb'=2,'c'=2,'zh'=4,'y'=4] {'c'}, dimensions={0} | all-to-all | bytes 4194304 | tf_op jit(solution)/shard_map/all_to_all | solution.py:20
  13.2 0.0 copy-done.6
  13.2 0.0 copy-start
  13.2 0.0 copy-start.1
  13.2 2.6 %shard_map.46 = (bf16[16,16,1152]{2,1,0:T(8,128)(2,1)}, f32[1024,128]{1,0:T(8,128)S(1)}) custom-call(bf16[2,512,1024]{2,1,0:T(8,128)(2,1)S(1)} %all_to_all.20.tok_ref, bf16[1024,128]{1,0:T(8,128)(2,1)S(1)} %copy-done.6), custom_call_target="tpu_custom_call" | custom-call | tf_op jit(solution)/shard_map/pallas_call | solution.py:203
  15.8 3.6 %all-to-all-start.1 = ((bf16[16,16,1152]{2,1,0:T(8,128)(2,1)}), bf16[16,16,1152]{2,1,0:T(8,128)(2,1)S(1)}, u32[]{:S(2)}, u32[]{:S(2)}) async-start(bf16[16,16,1152]{2,1,0:T(8,128)(2,1)} %get-tuple-element.22), calls=%async_computation.1 | async-start | bytes 1179648 | tf_op jit(solution)/shard_map/all_to_all | solution.py:20
  19.4 0.0 copy-done
  19.4 2.3 %collective-permute-start = (bf16[1,1024,512]{2,1,0:T(8,128)(2,1)S(1)}, bf16[1,1024,512]{2,1,0:T(8,128)(2,1)S(1)}, u32[]{:S(2)}, u32[]{:S(2)}) collective-permute-start(bf16[1,1024,512]{2,1,0:T(8,128)(2,1)S(1)} %copy-done), channel_id=1, source_target_pairs={{0,16},{16,0},{1,17},{17,1},{2,18},{18,2},{3,19},{19,3},{4,20},{20... | collective-permute-start | bytes 3145736 | tf_op jit(solution)/shard_map/ppermute | solution.py:239
  21.7 0.0 copy-done.1
  21.7 2.0 %collective-permute-start.1 = (bf16[1,512,1024]{2,1,0:T(8,128)(2,1)S(1)}, bf16[1,512,1024]{2,1,0:T(8,128)(2,1)S(1)}, u32[]{:S(2)}, u32[]{:S(2)}) collective-permute-start(bf16[1,512,1024]{2,1,0:T(8,128)(2,1)S(1)} %copy-done.1), channel_id=1, source_target_pairs={{0,16},{16,0},{1,17},{17,1},{2,18},{18,2},{3,19},{19,3},{4,20},{20... | collective-permute-start | bytes 3145736 | tf_op jit(solution)/shard_map/ppermute | solution.py:240
  23.8 0.2 collective-permute-done.a2_hbm
  24.0 0.0 copy-start.2
  24.0 1.0 copy-done.2
  25.0 1.3 %collective-permute-done.1.b2_hbm = bf16[1,512,1024]{2,1,0:T(8,128)(2,1)S(1)} collective-permute-done((bf16[1,512,1024]{2,1,0:T(8,128)(2,1)S(1)}, bf16[1,512,1024]{2,1,0:T(8,128)(2,1)S(1)}, u32[]{:S(2)}, u32[]{:S(2)}) %collective-permute-start.1) | collective-permute-done | bytes 1048608 | tf_op jit(solution)/shard_map/ppermute | solution.py:240
  26.3 0.0 copy-start.4
  26.3 1.0 copy-done.4
  27.2 9.5 %all-to-all-done.1.got_ref = bf16[16,16,1152]{2,1,0:T(8,128)(2,1)S(1)} async-done(((bf16[16,16,1152]{2,1,0:T(8,128)(2,1)}), bf16[16,16,1152]{2,1,0:T(8,128)(2,1)S(1)}, u32[]{:S(2)}, u32[]{:S(2)}) %all-to-all-start.1) | async-done | bytes 589856 | tf_op jit(solution)/shard_map/all_to_all | solution.py:20
  36.7 0.0 copy-start.3
  36.7 1.2 %copy-done.3 = bf16[1,1024,512]{2,1,0:T(8,128)(2,1)S(1)} copy-done((bf16[1,1024,512]{2,1,0:T(8,128)(2,1)S(1)}, bf16[1,1024,512]{2,1,0:T(8,128)(2,1)}, u32[]{:S(2)}) %copy-start.3) | copy-done | bytes 1048600
  37.9 0.0 copy-start.5
  37.9 1.2 %copy-done.5 = bf16[1,512,1024]{2,1,0:T(8,128)(2,1)S(1)} copy-done((bf16[1,512,1024]{2,1,0:T(8,128)(2,1)S(1)}, bf16[1,512,1024]{2,1,0:T(8,128)(2,1)}, u32[]{:S(2)}) %copy-start.5) | copy-done | bytes 1048600
  39.2 2.0 %shard_map.47 = bf16[4,16,1024]{2,1,0:T(8,128)(2,1)} custom-call(bf16[16,16,1152]{2,1,0:T(8,128)(2,1)S(1)} %all-to-all-done.1.got_ref, bf16[1,1024,512]{2,1,0:T(8,128)(2,1)S(1)} %copy-done, bf16[1,512,1024]{2,1,0:T(8,128)(2,1)S(1)} %copy-done.1, bf16[1,1024,512]{2,1,0:T(8,128)(2,1)S(1)} %copy-done.3, bf16[1,512,1024]{2,1,0:T(8,128)(2,1)S(1)} %copy-done.5), custom_call_target="tpu_custom_call" | custom-call | tf_op jit(solution)/shard_map/pallas_call | solution.py:203
  41.2 3.3 %all-to-all-start.2 = ((bf16[4,16,1024]{2,1,0:T(8,128)(2,1)}), bf16[4,16,1024]{2,1,0:T(8,128)(2,1)S(1)}, u32[]{:S(2)}, u32[]{:S(2)}) async-start(bf16[4,16,1024]{2,1,0:T(8,128)(2,1)} %shard_map.47), calls=%async_computation.2 | async-start | bytes 262144 | tf_op jit(solution)/shard_map/all_to_all | solution.py:20
  44.6 0.1 pad_add_fusion.at_ref
  44.6 0.8 shard_map.49
  45.4 2.3 %collective-permute-start.2 = (bf16[272,128]{1,0:T(8,128)(2,1)S(1)}, bf16[272,128]{1,0:T(8,128)(2,1)S(1)}, u32[]{:S(2)}, u32[]{:S(2)}) collective-permute-start(bf16[272,128]{1,0:T(8,128)(2,1)S(1)} %get-tuple-element.25), channel_id=1, source_target_pairs={{0,1},{1,0},{2,3},{3,2},{4,5},{5,4},{6,7},{7,6},{8,9},{9,8},{10,11... | collective-permute-start | bytes 208904 | tf_op jit(solution)/shard_map/ppermute | solution.py:254
  47.8 4.5 %collective-permute-start.3 = (bf16[272,128]{1,0:T(8,128)(2,1)S(1)}, bf16[272,128]{1,0:T(8,128)(2,1)S(1)}, u32[]{:S(2)}, u32[]{:S(2)}) collective-permute-start(bf16[272,128]{1,0:T(8,128)(2,1)S(1)} %get-tuple-element.26), channel_id=1, source_target_pairs={{0,2},{1,3},{2,0},{3,1},{4,6},{5,7},{6,4},{7,5},{8,10},{9,11},{10,... | collective-permute-start | bytes 208904 | tf_op jit(solution)/shard_map/ppermute | solution.py:254
  52.3 2.7 %collective-permute-start.4 = (bf16[272,128]{1,0:T(8,128)(2,1)S(1)}, bf16[272,128]{1,0:T(8,128)(2,1)S(1)}, u32[]{:S(2)}, u32[]{:S(2)}) collective-permute-start(bf16[272,128]{1,0:T(8,128)(2,1)S(1)} %get-tuple-element.27), channel_id=1, source_target_pairs={{0,3},{1,2},{2,1},{3,0},{4,7},{5,6},{6,5},{7,4},{8,11},{9,10},{10,... | collective-permute-start | bytes 208904 | tf_op jit(solution)/shard_map/ppermute | solution.py:254
  55.0 0.0 all-to-all-done.2.got_ref
  55.1 0.1 shard_map.48
  55.2 0.0 collective-permute-done.2.r1
  55.2 0.0 collective-permute-done.3.r2
  55.2 3.4 %collective-permute-done.4.r3 = bf16[272,128]{1,0:T(8,128)(2,1)S(1)} collective-permute-done((bf16[272,128]{1,0:T(8,128)(2,1)S(1)}, bf16[272,128]{1,0:T(8,128)(2,1)S(1)}, u32[]{:S(2)}, u32[]{:S(2)}) %collective-permute-start.4) | collective-permute-done | bytes 69664 | tf_op jit(solution)/shard_map/ppermute | solution.py:254
  58.6 16.1 %all_to_all.21 = bf16[16,32,1024]{2,1,0:T(8,128)(2,1)S(1)} all-to-all(bf16[16,32,1024]{2,1,0:T(8,128)(2,1)S(1)} %shard_map.48), channel_id=1, replica_groups=mesh['x'=4,'zla'=2,'zlb'=2,'c'=2,'zh'=4,'y'=4] {'x','y'}, dimensions={0} | all-to-all | bytes 2097152 | tf_op jit(solution)/shard_map/all_to_all | solution.py:20
  74.7 1.4 %shard_map.50 = (bf16[2,264,128]{2,1,0:T(8,128)(2,1)S(1)}, bf16[2,264,128]{2,1,0:T(8,128)(2,1)S(1)}, bf16[2,264,128]{2,1,0:T(8,128)(2,1)S(1)}, bf16[2,264,128]{2,1,0:T(8,128)(2,1)S(1)}) custom-call(s32[3]{0:T(128)S(1)} %pad_add_fusion.at_ref, bf16[272,128]{1,0:T(8,128)(2,1)S(1)} %get-tuple-element.28.r0, bf16[272,128]{1,0:T(8,128)(2,1)S(1)} %collective-permute-done.2.r1, ...), custom_call_target="tpu_custom_call" | custom-call | tf_op jit(solution)/shard_map/pallas_call | solution.py:203
  76.1 8.8 %collective-permute-start.5 = (bf16[2,264,128]{2,1,0:T(8,128)(2,1)S(1)}, bf16[2,264,128]{2,1,0:T(8,128)(2,1)S(1)}, u32[]{:S(2)}, u32[]{:S(2)}) collective-permute-start(bf16[2,264,128]{2,1,0:T(8,128)(2,1)S(1)} %get-tuple-element.34), channel_id=1, source_target_pairs={{0,4},{4,0},{8,12},{12,8},{1,5},{5,1},{9,13},{13,9},{2,6},{6,2},{1... | collective-permute-start | bytes 405512 | tf_op jit(solution)/shard_map/ppermute | solution.py:284
  84.9 7.9 %collective-permute-start.6 = (bf16[2,264,128]{2,1,0:T(8,128)(2,1)S(1)}, bf16[2,264,128]{2,1,0:T(8,128)(2,1)S(1)}, u32[]{:S(2)}, u32[]{:S(2)}) collective-permute-start(bf16[2,264,128]{2,1,0:T(8,128)(2,1)S(1)} %get-tuple-element.35), channel_id=1, source_target_pairs={{0,8},{4,12},{8,0},{12,4},{1,9},{5,13},{9,1},{13,5},{2,10},{6,14},... | collective-permute-start | bytes 405512 | tf_op jit(solution)/shard_map/ppermute | solution.py:284
  92.8 1.9 %collective-permute-start.7 = (bf16[2,264,128]{2,1,0:T(8,128)(2,1)S(1)}, bf16[2,264,128]{2,1,0:T(8,128)(2,1)S(1)}, u32[]{:S(2)}, u32[]{:S(2)}) collective-permute-start(bf16[2,264,128]{2,1,0:T(8,128)(2,1)S(1)} %get-tuple-element.36), channel_id=1, source_target_pairs={{0,12},{4,8},{8,4},{12,0},{1,13},{5,9},{9,5},{13,1},{2,14},{6,10},... | collective-permute-start | bytes 405512 | tf_op jit(solution)/shard_map/ppermute | solution.py:284
  94.8 1.8 %collective-permute-done.5.refs_1_ = bf16[2,264,128]{2,1,0:T(8,128)(2,1)S(1)} collective-permute-done((bf16[2,264,128]{2,1,0:T(8,128)(2,1)S(1)}, bf16[2,264,128]{2,1,0:T(8,128)(2,1)S(1)}, u32[]{:S(2)}, u32[]{:S(2)}) %collective-permute-start.5) | collective-permute-done | bytes 135200 | tf_op jit(solution)/shard_map/ppermute | solution.py:284
  96.5 3.5 %collective-permute-done.6.refs_2_ = bf16[2,264,128]{2,1,0:T(8,128)(2,1)S(1)} collective-permute-done((bf16[2,264,128]{2,1,0:T(8,128)(2,1)S(1)}, bf16[2,264,128]{2,1,0:T(8,128)(2,1)S(1)}, u32[]{:S(2)}, u32[]{:S(2)}) %collective-permute-start.6) | collective-permute-done | bytes 135200 | tf_op jit(solution)/shard_map/ppermute | solution.py:284
  100.1 15.2 %collective-permute-done.7.refs_3_ = bf16[2,264,128]{2,1,0:T(8,128)(2,1)S(1)} collective-permute-done((bf16[2,264,128]{2,1,0:T(8,128)(2,1)S(1)}, bf16[2,264,128]{2,1,0:T(8,128)(2,1)S(1)}, u32[]{:S(2)}, u32[]{:S(2)}) %collective-permute-start.7) | collective-permute-done | bytes 135200 | tf_op jit(solution)/shard_map/ppermute | solution.py:284
  115.3 0.7 shard_map.51
  116.0 4.3 %all-gather = bf16[64,1024]{1,0:T(8,128)(2,1)S(1)} all-gather(bf16[32,1024]{1,0:T(8,128)(2,1)S(1)} %get-tuple-element.38), channel_id=2, replica_groups=mesh['x'=4,'zla'=2,'zlb'=2,'c'=2,'zh'=4,'y'=4] {'c'}, dimensions={0}, use_global_device_ids=true | all-gather | bytes 196608 | tf_op jit(solution)/shard_map/all_gather | solution.py:288
  120.2 1.2 shard_map.52
Async XLA Ops:
  0.0 13.2 %copy-start.6 = (bf16[1024,128]{1,0:T(8,128)(2,1)S(1)}, bf16[1024,128]{1,0:T(8,128)(2,1)}, u32[]{:S(2)}) copy-start(bf16[1024,128]{1,0:T(8,128)(2,1)} %router_ref.1) | copy-start | bytes 786436
  13.2 6.2 %copy-start = (bf16[1,1024,512]{2,1,0:T(8,128)(2,1)S(1)}, bf16[1,1024,512]{2,1,0:T(8,128)(2,1)}, u32[]{:S(2)}) copy-start(bf16[1,1024,512]{2,1,0:T(8,128)(2,1)} %a_ref.1) | copy-start | bytes 3145732
  13.2 8.5 %copy-start.1 = (bf16[1,512,1024]{2,1,0:T(8,128)(2,1)S(1)}, bf16[1,512,1024]{2,1,0:T(8,128)(2,1)}, u32[]{:S(2)}) copy-start(bf16[1,512,1024]{2,1,0:T(8,128)(2,1)} %b_ref.1) | copy-start | bytes 3145732
  15.8 20.9 %all-to-all-start.1 = ((bf16[16,16,1152]{2,1,0:T(8,128)(2,1)}), bf16[16,16,1152]{2,1,0:T(8,128)(2,1)S(1)}, u32[]{:S(2)}, u32[]{:S(2)}) async-start(bf16[16,16,1152]{2,1,0:T(8,128)(2,1)} %get-tuple-element.22), calls=%async_computation.1 | async-start | bytes 1179648 | tf_op jit(solution)/shard_map/all_to_all | solution.py:20
  19.4 4.6 %collective-permute-start = (bf16[1,1024,512]{2,1,0:T(8,128)(2,1)S(1)}, bf16[1,1024,512]{2,1,0:T(8,128)(2,1)S(1)}, u32[]{:S(2)}, u32[]{:S(2)}) collective-permute-start(bf16[1,1024,512]{2,1,0:T(8,128)(2,1)S(1)} %copy-done), channel_id=1, source_target_pairs={{0,16},{16,0},{1,17},{17,1},{2,18},{18,2},{3,19},{19,3},{4,20},{20... | collective-permute-start | bytes 3145736 | tf_op jit(solution)/shard_map/ppermute | solution.py:239
  21.7 4.6 %collective-permute-start.1 = (bf16[1,512,1024]{2,1,0:T(8,128)(2,1)S(1)}, bf16[1,512,1024]{2,1,0:T(8,128)(2,1)S(1)}, u32[]{:S(2)}, u32[]{:S(2)}) collective-permute-start(bf16[1,512,1024]{2,1,0:T(8,128)(2,1)S(1)} %copy-done.1), channel_id=1, source_target_pairs={{0,16},{16,0},{1,17},{17,1},{2,18},{18,2},{3,19},{19,3},{4,20},{20... | collective-permute-start | bytes 3145736 | tf_op jit(solution)/shard_map/ppermute | solution.py:240
  24.0 1.0 copy-start.2
  26.3 1.0 copy-start.4
  36.7 1.2 %copy-start.3 = (bf16[1,1024,512]{2,1,0:T(8,128)(2,1)S(1)}, bf16[1,1024,512]{2,1,0:T(8,128)(2,1)}, u32[]{:S(2)}) copy-start(bf16[1,1024,512]{2,1,0:T(8,128)(2,1)} %copy-done.2) | copy-start | bytes 3145732
  37.9 1.2 %copy-start.5 = (bf16[1,512,1024]{2,1,0:T(8,128)(2,1)S(1)}, bf16[1,512,1024]{2,1,0:T(8,128)(2,1)}, u32[]{:S(2)}) copy-start(bf16[1,512,1024]{2,1,0:T(8,128)(2,1)} %copy-done.4) | copy-start | bytes 3145732
  41.2 13.8 %all-to-all-start.2 = ((bf16[4,16,1024]{2,1,0:T(8,128)(2,1)}), bf16[4,16,1024]{2,1,0:T(8,128)(2,1)S(1)}, u32[]{:S(2)}, u32[]{:S(2)}) async-start(bf16[4,16,1024]{2,1,0:T(8,128)(2,1)} %shard_map.47), calls=%async_computation.2 | async-start | bytes 262144 | tf_op jit(solution)/shard_map/all_to_all | solution.py:20
  45.4 9.7 %collective-permute-start.2 = (bf16[272,128]{1,0:T(8,128)(2,1)S(1)}, bf16[272,128]{1,0:T(8,128)(2,1)S(1)}, u32[]{:S(2)}, u32[]{:S(2)}) collective-permute-start(bf16[272,128]{1,0:T(8,128)(2,1)S(1)} %get-tuple-element.25), channel_id=1, source_target_pairs={{0,1},{1,0},{2,3},{3,2},{4,5},{5,4},{6,7},{7,6},{8,9},{9,8},{10,11... | collective-permute-start | bytes 208904 | tf_op jit(solution)/shard_map/ppermute | solution.py:254
  47.8 7.4 %collective-permute-start.3 = (bf16[272,128]{1,0:T(8,128)(2,1)S(1)}, bf16[272,128]{1,0:T(8,128)(2,1)S(1)}, u32[]{:S(2)}, u32[]{:S(2)}) collective-permute-start(bf16[272,128]{1,0:T(8,128)(2,1)S(1)} %get-tuple-element.26), channel_id=1, source_target_pairs={{0,2},{1,3},{2,0},{3,1},{4,6},{5,7},{6,4},{7,5},{8,10},{9,11},{10,... | collective-permute-start | bytes 208904 | tf_op jit(solution)/shard_map/ppermute | solution.py:254
  52.3 6.3 %collective-permute-start.4 = (bf16[272,128]{1,0:T(8,128)(2,1)S(1)}, bf16[272,128]{1,0:T(8,128)(2,1)S(1)}, u32[]{:S(2)}, u32[]{:S(2)}) collective-permute-start(bf16[272,128]{1,0:T(8,128)(2,1)S(1)} %get-tuple-element.27), channel_id=1, source_target_pairs={{0,3},{1,2},{2,1},{3,0},{4,7},{5,6},{6,5},{7,4},{8,11},{9,10},{10,... | collective-permute-start | bytes 208904 | tf_op jit(solution)/shard_map/ppermute | solution.py:254
  76.1 20.5 %collective-permute-start.5 = (bf16[2,264,128]{2,1,0:T(8,128)(2,1)S(1)}, bf16[2,264,128]{2,1,0:T(8,128)(2,1)S(1)}, u32[]{:S(2)}, u32[]{:S(2)}) collective-permute-start(bf16[2,264,128]{2,1,0:T(8,128)(2,1)S(1)} %get-tuple-element.34), channel_id=1, source_target_pairs={{0,4},{4,0},{8,12},{12,8},{1,5},{5,1},{9,13},{13,9},{2,6},{6,2},{1... | collective-permute-start | bytes 405512 | tf_op jit(solution)/shard_map/ppermute | solution.py:284
  84.9 15.2 %collective-permute-start.6 = (bf16[2,264,128]{2,1,0:T(8,128)(2,1)S(1)}, bf16[2,264,128]{2,1,0:T(8,128)(2,1)S(1)}, u32[]{:S(2)}, u32[]{:S(2)}) collective-permute-start(bf16[2,264,128]{2,1,0:T(8,128)(2,1)S(1)} %get-tuple-element.35), channel_id=1, source_target_pairs={{0,8},{4,12},{8,0},{12,4},{1,9},{5,13},{9,1},{13,5},{2,10},{6,14},... | collective-permute-start | bytes 405512 | tf_op jit(solution)/shard_map/ppermute | solution.py:284
  92.8 22.4 %collective-permute-start.7 = (bf16[2,264,128]{2,1,0:T(8,128)(2,1)S(1)}, bf16[2,264,128]{2,1,0:T(8,128)(2,1)S(1)}, u32[]{:S(2)}, u32[]{:S(2)}) collective-permute-start(bf16[2,264,128]{2,1,0:T(8,128)(2,1)S(1)} %get-tuple-element.36), channel_id=1, source_target_pairs={{0,12},{4,8},{8,4},{12,0},{1,13},{5,9},{9,5},{13,1},{2,14},{6,10},... | collective-permute-start | bytes 405512 | tf_op jit(solution)/shard_map/ppermute | solution.py:284

commit v5 on v4

--- a/solution.py
+++ b/solution.py
@@ -99,15 +99,15 @@
         copy.start()
     rows = blend(got_ref, [(k,) for k in range(got_ref.shape[0])]).astype(bf16)
 
-    def part(a, b):
+    def first(a):
         hidden = jnp.dot(rows, a[0], preferred_element_type=f32)
-        hidden = jax.nn.gelu(hidden, approximate=True).astype(bf16)
-        return jnp.dot(hidden, b[0], preferred_element_type=f32)
-
-    out = part(a_ref, b_ref)
-    for copy in copies:
-        copy.wait()
-    out = (out + part(a2_ref, b2_ref)).astype(bf16)
+        return jax.nn.gelu(hidden, approximate=True).astype(bf16)
+
+    out = jnp.dot(first(a_ref), b_ref[0], preferred_element_type=f32)
+    copies[0].wait()
+    hidden = first(a2_ref)
+    copies[1].wait()
+    out = (out + jnp.dot(hidden, b2_ref[0], preferred_element_type=f32)).astype(bf16)
     for k in range(out_ref.shape[0]):
         out_ref[k] = out
 

time: 122 us -> 122 us (level)
  no operation moved by 1% of the time
where the time goes in v5:
time: 122 us; the launch traced here: 121 us
  starting transfers between devices  39.5 us (32%)
  waiting for transfers between devices  34.9 us (29%)
  blocking collectives  33.6 us (28%)
  Pallas kernels  8.82 us (7%)
  local copies, waits for them, and re-layouts  4.43 us (4%)
    all_to_all x2, blocking collectives, swap(): return lax.all_to_all(tiles, axis, split_axis=0, concat_axis=0, tiled=True)  29.3 us
    ppermute x3, waiting for transfers between devices, shards(): outs[k] = lax.ppermute(outs[k], 'zh', [(i, i ^ k) for i in range(nzh)])  20.5 us
    ppermute x3, starting transfers between devices, shards(): outs[k] = lax.ppermute(outs[k], 'zh', [(i, i ^ k) for i in range(nzh)])  18.7 us
    ppermute x3, starting transfers between devices, shards(): rows[k] = lax.ppermute(rows[k], 'y', [(i, i ^ k) for i in range(ny)])  9.58 us
    all_to_all x2, waiting for transfers between devices, swap(): return lax.all_to_all(tiles, axis, split_axis=0, concat_axis=0, tiled=True)  9.47 us
    pallas_call x7, Pallas kernels, call(): pl.pallas_call(kernel, out_shape=outs, in_specs=specs, out_specs=jax.tree...  8.82 us
    all_to_all x2, starting transfers between devices, swap(): return lax.all_to_all(tiles, axis, split_axis=0, concat_axis=0, tiled=True)  6.92 us
    unnamed x14, local copies, waits for them, and re-layouts  4.43 us
  transfers between devices with their start and end apart: 10, of which 7 were waited for; matrix products, arithmetic and copies ran while one was open for 0% of the time, Pallas kernels for 1%

profile of v5, /device:TPU:1, one launch (start us, length us, event | category | flops | bytes accessed | tf_op | source)
XLA Modules:
  0.0 121.5 jit_solution(2679911616426155395)
XLA Ops:
  0.0 0.0 copy-start.6
  0.0 13.2 %all_to_all.20.tok_ref = bf16[2,512,1024]{2,1,0:T(8,128)(2,1)S(1)} all-to-all(bf16[2,512,1024]{2,1,0:T(8,128)(2,1)} %param.4), channel_id=1, replica_groups=mesh['x'=4,'zla'=2,'zlb'=2,'c'=2,'zh'=4,'y'=4] {'c'}, dimensions={0} | all-to-all | bytes 4194304 | tf_op jit(solution)/shard_map/all_to_all | solution.py:20
  13.2 0.0 copy-done.6
  13.2 0.0 copy-start
  13.2 0.0 copy-start.1
  13.2 2.6 %shard_map.46 = (bf16[16,16,1152]{2,1,0:T(8,128)(2,1)}, f32[1024,128]{1,0:T(8,128)S(1)}) custom-call(bf16[2,512,1024]{2,1,0:T(8,128)(2,1)S(1)} %all_to_all.20.tok_ref, bf16[1024,128]{1,0:T(8,128)(2,1)S(1)} %copy-done.6), custom_call_target="tpu_custom_call" | custom-call | tf_op jit(solution)/shard_map/pallas_call | solution.py:203
  15.8 3.6 %all-to-all-start.1 = ((bf16[16,16,1152]{2,1,0:T(8,128)(2,1)}), bf16[16,16,1152]{2,1,0:T(8,128)(2,1)S(1)}, u32[]{:S(2)}, u32[]{:S(2)}) async-start(bf16[16,16,1152]{2,1,0:T(8,128)(2,1)} %get-tuple-element.22), calls=%async_computation.1 | async-start | bytes 1179648 | tf_op jit(solution)/shard_map/all_to_all | solution.py:20
  19.4 0.0 copy-done
  19.4 2.3 %collective-permute-start = (bf16[1,1024,512]{2,1,0:T(8,128)(2,1)S(1)}, bf16[1,1024,512]{2,1,0:T(8,128)(2,1)S(1)}, u32[]{:S(2)}, u32[]{:S(2)}) collective-permute-start(bf16[1,1024,512]{2,1,0:T(8,128)(2,1)S(1)} %copy-done), channel_id=1, source_target_pairs={{0,16},{16,0},{1,17},{17,1},{2,18},{18,2},{3,19},{19,3},{4,20},{20... | collective-permute-start | bytes 3145736 | tf_op jit(solution)/shard_map/ppermute | solution.py:239
  21.7 0.0 copy-done.1
  21.7 2.0 %collective-permute-start.1 = (bf16[1,512,1024]{2,1,0:T(8,128)(2,1)S(1)}, bf16[1,512,1024]{2,1,0:T(8,128)(2,1)S(1)}, u32[]{:S(2)}, u32[]{:S(2)}) collective-permute-start(bf16[1,512,1024]{2,1,0:T(8,128)(2,1)S(1)} %copy-done.1), channel_id=1, source_target_pairs={{0,16},{16,0},{1,17},{17,1},{2,18},{18,2},{3,19},{19,3},{4,20},{20... | collective-permute-start | bytes 3145736 | tf_op jit(solution)/shard_map/ppermute | solution.py:240
  23.8 0.2 collective-permute-done.a2_hbm
  24.0 0.0 copy-start.2
  24.0 1.0 copy-done.2
  25.0 1.3 %collective-permute-done.1.b2_hbm = bf16[1,512,1024]{2,1,0:T(8,128)(2,1)S(1)} collective-permute-done((bf16[1,512,1024]{2,1,0:T(8,128)(2,1)S(1)}, bf16[1,512,1024]{2,1,0:T(8,128)(2,1)S(1)}, u32[]{:S(2)}, u32[]{:S(2)}) %collective-permute-start.1) | collective-permute-done | bytes 1048608 | tf_op jit(solution)/shard_map/ppermute | solution.py:240
  26.3 0.0 copy-start.4
  26.3 1.0 copy-done.4
  27.2 9.5 %all-to-all-done.1.got_ref = bf16[16,16,1152]{2,1,0:T(8,128)(2,1)S(1)} async-done(((bf16[16,16,1152]{2,1,0:T(8,128)(2,1)}), bf16[16,16,1152]{2,1,0:T(8,128)(2,1)S(1)}, u32[]{:S(2)}, u32[]{:S(2)}) %all-to-all-start.1) | async-done | bytes 589856 | tf_op jit(solution)/shard_map/all_to_all | solution.py:20
  36.7 0.0 copy-start.3
  36.7 1.2 %copy-done.3 = bf16[1,1024,512]{2,1,0:T(8,128)(2,1)S(1)} copy-done((bf16[1,1024,512]{2,1,0:T(8,128)(2,1)S(1)}, bf16[1,1024,512]{2,1,0:T(8,128)(2,1)}, u32[]{:S(2)}) %copy-start.3) | copy-done | bytes 1048600
  37.9 0.0 copy-start.5
  37.9 1.2 %copy-done.5 = bf16[1,512,1024]{2,1,0:T(8,128)(2,1)S(1)} copy-done((bf16[1,512,1024]{2,1,0:T(8,128)(2,1)S(1)}, bf16[1,512,1024]{2,1,0:T(8,128)(2,1)}, u32[]{:S(2)}) %copy-start.5) | copy-done | bytes 1048600
  39.2 2.1 %shard_map.47 = bf16[4,16,1024]{2,1,0:T(8,128)(2,1)} custom-call(bf16[16,16,1152]{2,1,0:T(8,128)(2,1)S(1)} %all-to-all-done.1.got_ref, bf16[1,1024,512]{2,1,0:T(8,128)(2,1)S(1)} %copy-done, bf16[1,512,1024]{2,1,0:T(8,128)(2,1)S(1)} %copy-done.1, bf16[1,1024,512]{2,1,0:T(8,128)(2,1)S(1)} %copy-done.3, bf16[1,512,1024]{2,1,0:T(8,128)(2,1)S(1)} %copy-done.5), custom_call_target="tpu_custom_call" | custom-call | tf_op jit(solution)/shard_map/pallas_call | solution.py:203
  41.2 3.3 %all-to-all-start.2 = ((bf16[4,16,1024]{2,1,0:T(8,128)(2,1)}), bf16[4,16,1024]{2,1,0:T(8,128)(2,1)S(1)}, u32[]{:S(2)}, u32[]{:S(2)}) async-start(bf16[4,16,1024]{2,1,0:T(8,128)(2,1)} %shard_map.47), calls=%async_computation.2 | async-start | bytes 262144 | tf_op jit(solution)/shard_map/all_to_all | solution.py:20
  44.6 0.1 pad_add_fusion.at_ref
  44.7 0.8 shard_map.49
  45.5 2.3 %collective-permute-start.2 = (bf16[272,128]{1,0:T(8,128)(2,1)S(1)}, bf16[272,128]{1,0:T(8,128)(2,1)S(1)}, u32[]{:S(2)}, u32[]{:S(2)}) collective-permute-start(bf16[272,128]{1,0:T(8,128)(2,1)S(1)} %get-tuple-element.25), channel_id=1, source_target_pairs={{0,1},{1,0},{2,3},{3,2},{4,5},{5,4},{6,7},{7,6},{8,9},{9,8},{10,11... | collective-permute-start | bytes 208904 | tf_op jit(solution)/shard_map/ppermute | solution.py:254
  47.8 4.5 %collective-permute-start.3 = (bf16[272,128]{1,0:T(8,128)(2,1)S(1)}, bf16[272,128]{1,0:T(8,128)(2,1)S(1)}, u32[]{:S(2)}, u32[]{:S(2)}) collective-permute-start(bf16[272,128]{1,0:T(8,128)(2,1)S(1)} %get-tuple-element.26), channel_id=1, source_target_pairs={{0,2},{1,3},{2,0},{3,1},{4,6},{5,7},{6,4},{7,5},{8,10},{9,11},{10,... | collective-permute-start | bytes 208904 | tf_op jit(solution)/shard_map/ppermute | solution.py:254
  52.4 2.7 %collective-permute-start.4 = (bf16[272,128]{1,0:T(8,128)(2,1)S(1)}, bf16[272,128]{1,0:T(8,128)(2,1)S(1)}, u32[]{:S(2)}, u32[]{:S(2)}) collective-permute-start(bf16[272,128]{1,0:T(8,128)(2,1)S(1)} %get-tuple-element.27), channel_id=1, source_target_pairs={{0,3},{1,2},{2,1},{3,0},{4,7},{5,6},{6,5},{7,4},{8,11},{9,10},{10,... | collective-permute-start | bytes 208904 | tf_op jit(solution)/shard_map/ppermute | solution.py:254
  55.1 0.0 all-to-all-done.2.got_ref
  55.1 0.1 shard_map.48
  55.2 0.0 collective-permute-done.2.r1
  55.2 0.0 collective-permute-done.3.r2
  55.2 3.4 %collective-permute-done.4.r3 = bf16[272,128]{1,0:T(8,128)(2,1)S(1)} collective-permute-done((bf16[272,128]{1,0:T(8,128)(2,1)S(1)}, bf16[272,128]{1,0:T(8,128)(2,1)S(1)}, u32[]{:S(2)}, u32[]{:S(2)}) %collective-permute-start.4) | collective-permute-done | bytes 69664 | tf_op jit(solution)/shard_map/ppermute | solution.py:254
  58.6 16.1 %all_to_all.21 = bf16[16,32,1024]{2,1,0:T(8,128)(2,1)S(1)} all-to-all(bf16[16,32,1024]{2,1,0:T(8,128)(2,1)S(1)} %shard_map.48), channel_id=1, replica_groups=mesh['x'=4,'zla'=2,'zlb'=2,'c'=2,'zh'=4,'y'=4] {'x','y'}, dimensions={0} | all-to-all | bytes 2097152 | tf_op jit(solution)/shard_map/all_to_all | solution.py:20
  74.7 1.4 %shard_map.50 = (bf16[2,264,128]{2,1,0:T(8,128)(2,1)S(1)}, bf16[2,264,128]{2,1,0:T(8,128)(2,1)S(1)}, bf16[2,264,128]{2,1,0:T(8,128)(2,1)S(1)}, bf16[2,264,128]{2,1,0:T(8,128)(2,1)S(1)}) custom-call(s32[3]{0:T(128)S(1)} %pad_add_fusion.at_ref, bf16[272,128]{1,0:T(8,128)(2,1)S(1)} %get-tuple-element.28.r0, bf16[272,128]{1,0:T(8,128)(2,1)S(1)} %collective-permute-done.2.r1, ...), custom_call_target="tpu_custom_call" | custom-call | tf_op jit(solution)/shard_map/pallas_call | solution.py:203
  76.1 8.8 %collective-permute-start.5 = (bf16[2,264,128]{2,1,0:T(8,128)(2,1)S(1)}, bf16[2,264,128]{2,1,0:T(8,128)(2,1)S(1)}, u32[]{:S(2)}, u32[]{:S(2)}) collective-permute-start(bf16[2,264,128]{2,1,0:T(8,128)(2,1)S(1)} %get-tuple-element.34), channel_id=1, source_target_pairs={{0,4},{4,0},{8,12},{12,8},{1,5},{5,1},{9,13},{13,9},{2,6},{6,2},{1... | collective-permute-start | bytes 405512 | tf_op jit(solution)/shard_map/ppermute | solution.py:284
  84.9 7.9 %collective-permute-start.6 = (bf16[2,264,128]{2,1,0:T(8,128)(2,1)S(1)}, bf16[2,264,128]{2,1,0:T(8,128)(2,1)S(1)}, u32[]{:S(2)}, u32[]{:S(2)}) collective-permute-start(bf16[2,264,128]{2,1,0:T(8,128)(2,1)S(1)} %get-tuple-element.35), channel_id=1, source_target_pairs={{0,8},{4,12},{8,0},{12,4},{1,9},{5,13},{9,1},{13,5},{2,10},{6,14},... | collective-permute-start | bytes 405512 | tf_op jit(solution)/shard_map/ppermute | solution.py:284
  92.9 1.9 %collective-permute-start.7 = (bf16[2,264,128]{2,1,0:T(8,128)(2,1)S(1)}, bf16[2,264,128]{2,1,0:T(8,128)(2,1)S(1)}, u32[]{:S(2)}, u32[]{:S(2)}) collective-permute-start(bf16[2,264,128]{2,1,0:T(8,128)(2,1)S(1)} %get-tuple-element.36), channel_id=1, source_target_pairs={{0,12},{4,8},{8,4},{12,0},{1,13},{5,9},{9,5},{13,1},{2,14},{6,10},... | collective-permute-start | bytes 405512 | tf_op jit(solution)/shard_map/ppermute | solution.py:284
  94.8 1.8 %collective-permute-done.5.refs_1_ = bf16[2,264,128]{2,1,0:T(8,128)(2,1)S(1)} collective-permute-done((bf16[2,264,128]{2,1,0:T(8,128)(2,1)S(1)}, bf16[2,264,128]{2,1,0:T(8,128)(2,1)S(1)}, u32[]{:S(2)}, u32[]{:S(2)}) %collective-permute-start.5) | collective-permute-done | bytes 135200 | tf_op jit(solution)/shard_map/ppermute | solution.py:284
  96.6 3.5 %collective-permute-done.6.refs_2_ = bf16[2,264,128]{2,1,0:T(8,128)(2,1)S(1)} collective-permute-done((bf16[2,264,128]{2,1,0:T(8,128)(2,1)S(1)}, bf16[2,264,128]{2,1,0:T(8,128)(2,1)S(1)}, u32[]{:S(2)}, u32[]{:S(2)}) %collective-permute-start.6) | collective-permute-done | bytes 135200 | tf_op jit(solution)/shard_map/ppermute | solution.py:284
  100.1 15.2 %collective-permute-done.7.refs_3_ = bf16[2,264,128]{2,1,0:T(8,128)(2,1)S(1)} collective-permute-done((bf16[2,264,128]{2,1,0:T(8,128)(2,1)S(1)}, bf16[2,264,128]{2,1,0:T(8,128)(2,1)S(1)}, u32[]{:S(2)}, u32[]{:S(2)}) %collective-permute-start.7) | collective-permute-done | bytes 135200 | tf_op jit(solution)/shard_map/ppermute | solution.py:284
  115.3 0.7 shard_map.51
  116.0 4.3 %all-gather = bf16[64,1024]{1,0:T(8,128)(2,1)S(1)} all-gather(bf16[32,1024]{1,0:T(8,128)(2,1)S(1)} %get-tuple-element.38), channel_id=2, replica_groups=mesh['x'=4,'zla'=2,'zlb'=2,'c'=2,'zh'=4,'y'=4] {'c'}, dimensions={0}, use_global_device_ids=true | all-gather | bytes 196608 | tf_op jit(solution)/shard_map/all_gather | solution.py:288
  120.3 1.2 shard_map.52
Async XLA Ops:
  0.0 13.2 %copy-start.6 = (bf16[1024,128]{1,0:T(8,128)(2,1)S(1)}, bf16[1024,128]{1,0:T(8,128)(2,1)}, u32[]{:S(2)}) copy-start(bf16[1024,128]{1,0:T(8,128)(2,1)} %router_ref.1) | copy-start | bytes 786436
  13.2 6.2 %copy-start = (bf16[1,1024,512]{2,1,0:T(8,128)(2,1)S(1)}, bf16[1,1024,512]{2,1,0:T(8,128)(2,1)}, u32[]{:S(2)}) copy-start(bf16[1,1024,512]{2,1,0:T(8,128)(2,1)} %a_ref.1) | copy-start | bytes 3145732
  13.2 8.5 %copy-start.1 = (bf16[1,512,1024]{2,1,0:T(8,128)(2,1)S(1)}, bf16[1,512,1024]{2,1,0:T(8,128)(2,1)}, u32[]{:S(2)}) copy-start(bf16[1,512,1024]{2,1,0:T(8,128)(2,1)} %b_ref.1) | copy-start | bytes 3145732
  15.8 20.9 %all-to-all-start.1 = ((bf16[16,16,1152]{2,1,0:T(8,128)(2,1)}), bf16[16,16,1152]{2,1,0:T(8,128)(2,1)S(1)}, u32[]{:S(2)}, u32[]{:S(2)}) async-start(bf16[16,16,1152]{2,1,0:T(8,128)(2,1)} %get-tuple-element.22), calls=%async_computation.1 | async-start | bytes 1179648 | tf_op jit(solution)/shard_map/all_to_all | solution.py:20
  19.4 4.6 %collective-permute-start = (bf16[1,1024,512]{2,1,0:T(8,128)(2,1)S(1)}, bf16[1,1024,512]{2,1,0:T(8,128)(2,1)S(1)}, u32[]{:S(2)}, u32[]{:S(2)}) collective-permute-start(bf16[1,1024,512]{2,1,0:T(8,128)(2,1)S(1)} %copy-done), channel_id=1, source_target_pairs={{0,16},{16,0},{1,17},{17,1},{2,18},{18,2},{3,19},{19,3},{4,20},{20... | collective-permute-start | bytes 3145736 | tf_op jit(solution)/shard_map/ppermute | solution.py:239
  21.7 4.6 %collective-permute-start.1 = (bf16[1,512,1024]{2,1,0:T(8,128)(2,1)S(1)}, bf16[1,512,1024]{2,1,0:T(8,128)(2,1)S(1)}, u32[]{:S(2)}, u32[]{:S(2)}) collective-permute-start(bf16[1,512,1024]{2,1,0:T(8,128)(2,1)S(1)} %copy-done.1), channel_id=1, source_target_pairs={{0,16},{16,0},{1,17},{17,1},{2,18},{18,2},{3,19},{19,3},{4,20},{20... | collective-permute-start | bytes 3145736 | tf_op jit(solution)/shard_map/ppermute | solution.py:240
  24.0 1.0 copy-start.2
  26.3 1.0 copy-start.4
  36.7 1.2 %copy-start.3 = (bf16[1,1024,512]{2,1,0:T(8,128)(2,1)S(1)}, bf16[1,1024,512]{2,1,0:T(8,128)(2,1)}, u32[]{:S(2)}) copy-start(bf16[1,1024,512]{2,1,0:T(8,128)(2,1)} %copy-done.2) | copy-start | bytes 3145732
  37.9 1.2 %copy-start.5 = (bf16[1,512,1024]{2,1,0:T(8,128)(2,1)S(1)}, bf16[1,512,1024]{2,1,0:T(8,128)(2,1)}, u32[]{:S(2)}) copy-start(bf16[1,512,1024]{2,1,0:T(8,128)(2,1)} %copy-done.4) | copy-start | bytes 3145732
  41.2 13.8 %all-to-all-start.2 = ((bf16[4,16,1024]{2,1,0:T(8,128)(2,1)}), bf16[4,16,1024]{2,1,0:T(8,128)(2,1)S(1)}, u32[]{:S(2)}, u32[]{:S(2)}) async-start(bf16[4,16,1024]{2,1,0:T(8,128)(2,1)} %shard_map.47), calls=%async_computation.2 | async-start | bytes 262144 | tf_op jit(solution)/shard_map/all_to_all | solution.py:20
  45.5 9.7 %collective-permute-start.2 = (bf16[272,128]{1,0:T(8,128)(2,1)S(1)}, bf16[272,128]{1,0:T(8,128)(2,1)S(1)}, u32[]{:S(2)}, u32[]{:S(2)}) collective-permute-start(bf16[272,128]{1,0:T(8,128)(2,1)S(1)} %get-tuple-element.25), channel_id=1, source_target_pairs={{0,1},{1,0},{2,3},{3,2},{4,5},{5,4},{6,7},{7,6},{8,9},{9,8},{10,11... | collective-permute-start | bytes 208904 | tf_op jit(solution)/shard_map/ppermute | solution.py:254
  47.8 7.4 %collective-permute-start.3 = (bf16[272,128]{1,0:T(8,128)(2,1)S(1)}, bf16[272,128]{1,0:T(8,128)(2,1)S(1)}, u32[]{:S(2)}, u32[]{:S(2)}) collective-permute-start(bf16[272,128]{1,0:T(8,128)(2,1)S(1)} %get-tuple-element.26), channel_id=1, source_target_pairs={{0,2},{1,3},{2,0},{3,1},{4,6},{5,7},{6,4},{7,5},{8,10},{9,11},{10,... | collective-permute-start | bytes 208904 | tf_op jit(solution)/shard_map/ppermute | solution.py:254
  52.4 6.3 %collective-permute-start.4 = (bf16[272,128]{1,0:T(8,128)(2,1)S(1)}, bf16[272,128]{1,0:T(8,128)(2,1)S(1)}, u32[]{:S(2)}, u32[]{:S(2)}) collective-permute-start(bf16[272,128]{1,0:T(8,128)(2,1)S(1)} %get-tuple-element.27), channel_id=1, source_target_pairs={{0,3},{1,2},{2,1},{3,0},{4,7},{5,6},{6,5},{7,4},{8,11},{9,10},{10,... | collective-permute-start | bytes 208904 | tf_op jit(solution)/shard_map/ppermute | solution.py:254
  76.1 20.5 %collective-permute-start.5 = (bf16[2,264,128]{2,1,0:T(8,128)(2,1)S(1)}, bf16[2,264,128]{2,1,0:T(8,128)(2,1)S(1)}, u32[]{:S(2)}, u32[]{:S(2)}) collective-permute-start(bf16[2,264,128]{2,1,0:T(8,128)(2,1)S(1)} %get-tuple-element.34), channel_id=1, source_target_pairs={{0,4},{4,0},{8,12},{12,8},{1,5},{5,1},{9,13},{13,9},{2,6},{6,2},{1... | collective-permute-start | bytes 405512 | tf_op jit(solution)/shard_map/ppermute | solution.py:284
  84.9 15.2 %collective-permute-start.6 = (bf16[2,264,128]{2,1,0:T(8,128)(2,1)S(1)}, bf16[2,264,128]{2,1,0:T(8,128)(2,1)S(1)}, u32[]{:S(2)}, u32[]{:S(2)}) collective-permute-start(bf16[2,264,128]{2,1,0:T(8,128)(2,1)S(1)} %get-tuple-element.35), channel_id=1, source_target_pairs={{0,8},{4,12},{8,0},{12,4},{1,9},{5,13},{9,1},{13,5},{2,10},{6,14},... | collective-permute-start | bytes 405512 | tf_op jit(solution)/shard_map/ppermute | solution.py:284
  92.9 22.4 %collective-permute-start.7 = (bf16[2,264,128]{2,1,0:T(8,128)(2,1)S(1)}, bf16[2,264,128]{2,1,0:T(8,128)(2,1)S(1)}, u32[]{:S(2)}, u32[]{:S(2)}) collective-permute-start(bf16[2,264,128]{2,1,0:T(8,128)(2,1)S(1)} %get-tuple-element.36), channel_id=1, source_target_pairs={{0,12},{4,8},{8,4},{12,0},{1,13},{5,9},{9,5},{13,1},{2,14},{6,10},... | collective-permute-start | bytes 405512 | tf_op jit(solution)/shard_map/ppermute | solution.py:284

commit v6 on v4

--- a/solution.py
+++ b/solution.py
@@ -150,10 +150,14 @@
         rows = jnp.concatenate(in_three(top) + in_three(total) + [zero], axis=0)
         stats.append(rows)
     out = 0.0
-    for k in range(n):
-        y = at_ref[0] ^ k
-        block = found_ref[:, y].reshape(slots, width)
-        out = out + jnp.dot(jnp.concatenate(weights[k], axis=0), block, preferred_element_type=f32)
+    for k in range(0, n, 2):
+        both = [found_ref[:, at_ref[0] ^ i].reshape(slots, width) for i in (k, k + 1)]
+        left = [jnp.concatenate(weights[i], axis=0) for i in (k, k + 1)]
+        out = out + jnp.dot(
+            jnp.concatenate(left, axis=1),
+            jnp.concatenate(both, axis=0),
+            preferred_element_type=f32,
+        )
     out = out.astype(bf16)
     for c in range(cores):
         for z in range(nz):

time: 122 us -> 122 us (level)
  no operation moved by 1% of the time
where the time goes in v6:
time: 122 us; the launch traced here: 121 us
  starting transfers between devices  39.5 us (32%)
  waiting for transfers between devices  34.9 us (29%)
  blocking collectives  33.6 us (28%)
  Pallas kernels  8.53 us (7%)
  local copies, waits for them, and re-layouts  4.43 us (4%)
    all_to_all x2, blocking collectives, swap(): return lax.all_to_all(tiles, axis, split_axis=0, concat_axis=0, tiled=True)  29.3 us
    ppermute x3, waiting for transfers between devices, shards(): outs[k] = lax.ppermute(outs[k], 'zh', [(i, i ^ k) for i in range(nzh)])  20.5 us
    ppermute x3, starting transfers between devices, shards(): outs[k] = lax.ppermute(outs[k], 'zh', [(i, i ^ k) for i in range(nzh)])  18.7 us
    ppermute x3, starting transfers between devices, shards(): rows[k] = lax.ppermute(rows[k], 'y', [(i, i ^ k) for i in range(ny)])  9.58 us
    all_to_all x2, waiting for transfers between devices, swap(): return lax.all_to_all(tiles, axis, split_axis=0, concat_axis=0, tiled=True)  9.47 us
    pallas_call x7, Pallas kernels, call(): pl.pallas_call(kernel, out_shape=outs, in_specs=specs, out_specs=jax.tree...  8.53 us
    all_to_all x2, starting transfers between devices, swap(): return lax.all_to_all(tiles, axis, split_axis=0, concat_axis=0, tiled=True)  6.92 us
    unnamed x14, local copies, waits for them, and re-layouts  4.43 us
  transfers between devices with their start and end apart: 10, of which 7 were waited for; matrix products, arithmetic and copies ran while one was open for 0% of the time, Pallas kernels for 1%

profile of v6, /device:TPU:1, one launch (start us, length us, event | category | flops | bytes accessed | tf_op | source)
XLA Modules:
  0.0 121.2 jit_solution(12178718462311338338)
XLA Ops:
  0.0 0.0 copy-start.6
  0.0 13.2 %all_to_all.20.tok_ref = bf16[2,512,1024]{2,1,0:T(8,128)(2,1)S(1)} all-to-all(bf16[2,512,1024]{2,1,0:T(8,128)(2,1)} %param.4), channel_id=1, replica_groups=mesh['x'=4,'zla'=2,'zlb'=2,'c'=2,'zh'=4,'y'=4] {'c'}, dimensions={0} | all-to-all | bytes 4194304 | tf_op jit(solution)/shard_map/all_to_all | solution.py:20
  13.2 0.0 copy-done.6
  13.2 0.0 copy-start
  13.2 0.0 copy-start.1
  13.2 2.6 %shard_map.46 = (bf16[16,16,1152]{2,1,0:T(8,128)(2,1)}, f32[1024,128]{1,0:T(8,128)S(1)}) custom-call(bf16[2,512,1024]{2,1,0:T(8,128)(2,1)S(1)} %all_to_all.20.tok_ref, bf16[1024,128]{1,0:T(8,128)(2,1)S(1)} %copy-done.6), custom_call_target="tpu_custom_call" | custom-call | tf_op jit(solution)/shard_map/pallas_call | solution.py:207
  15.8 3.6 %all-to-all-start.1 = ((bf16[16,16,1152]{2,1,0:T(8,128)(2,1)}), bf16[16,16,1152]{2,1,0:T(8,128)(2,1)S(1)}, u32[]{:S(2)}, u32[]{:S(2)}) async-start(bf16[16,16,1152]{2,1,0:T(8,128)(2,1)} %get-tuple-element.22), calls=%async_computation.1 | async-start | bytes 1179648 | tf_op jit(solution)/shard_map/all_to_all | solution.py:20
  19.4 0.0 copy-done
  19.4 2.3 %collective-permute-start = (bf16[1,1024,512]{2,1,0:T(8,128)(2,1)S(1)}, bf16[1,1024,512]{2,1,0:T(8,128)(2,1)S(1)}, u32[]{:S(2)}, u32[]{:S(2)}) collective-permute-start(bf16[1,1024,512]{2,1,0:T(8,128)(2,1)S(1)} %copy-done), channel_id=1, source_target_pairs={{0,16},{16,0},{1,17},{17,1},{2,18},{18,2},{3,19},{19,3},{4,20},{20... | collective-permute-start | bytes 3145736 | tf_op jit(solution)/shard_map/ppermute | solution.py:243
  21.7 0.0 copy-done.1
  21.7 2.0 %collective-permute-start.1 = (bf16[1,512,1024]{2,1,0:T(8,128)(2,1)S(1)}, bf16[1,512,1024]{2,1,0:T(8,128)(2,1)S(1)}, u32[]{:S(2)}, u32[]{:S(2)}) collective-permute-start(bf16[1,512,1024]{2,1,0:T(8,128)(2,1)S(1)} %copy-done.1), channel_id=1, source_target_pairs={{0,16},{16,0},{1,17},{17,1},{2,18},{18,2},{3,19},{19,3},{4,20},{20... | collective-permute-start | bytes 3145736 | tf_op jit(solution)/shard_map/ppermute | solution.py:244
  23.8 0.2 collective-permute-done.a2_hbm
  24.0 0.0 copy-start.2
  24.0 1.0 copy-done.2
  25.0 1.3 %collective-permute-done.1.b2_hbm = bf16[1,512,1024]{2,1,0:T(8,128)(2,1)S(1)} collective-permute-done((bf16[1,512,1024]{2,1,0:T(8,128)(2,1)S(1)}, bf16[1,512,1024]{2,1,0:T(8,128)(2,1)S(1)}, u32[]{:S(2)}, u32[]{:S(2)}) %collective-permute-start.1) | collective-permute-done | bytes 1048608 | tf_op jit(solution)/shard_map/ppermute | solution.py:244
  26.3 0.0 copy-start.4
  26.3 1.0 copy-done.4
  27.2 9.5 %all-to-all-done.1.got_ref = bf16[16,16,1152]{2,1,0:T(8,128)(2,1)S(1)} async-done(((bf16[16,16,1152]{2,1,0:T(8,128)(2,1)}), bf16[16,16,1152]{2,1,0:T(8,128)(2,1)S(1)}, u32[]{:S(2)}, u32[]{:S(2)}) %all-to-all-start.1) | async-done | bytes 589856 | tf_op jit(solution)/shard_map/all_to_all | solution.py:20
  36.7 0.0 copy-start.3
  36.7 1.2 %copy-done.3 = bf16[1,1024,512]{2,1,0:T(8,128)(2,1)S(1)} copy-done((bf16[1,1024,512]{2,1,0:T(8,128)(2,1)S(1)}, bf16[1,1024,512]{2,1,0:T(8,128)(2,1)}, u32[]{:S(2)}) %copy-start.3) | copy-done | bytes 1048600
  37.9 0.0 copy-start.5
  37.9 1.2 %copy-done.5 = bf16[1,512,1024]{2,1,0:T(8,128)(2,1)S(1)} copy-done((bf16[1,512,1024]{2,1,0:T(8,128)(2,1)S(1)}, bf16[1,512,1024]{2,1,0:T(8,128)(2,1)}, u32[]{:S(2)}) %copy-start.5) | copy-done | bytes 1048600
  39.2 2.0 %shard_map.47 = bf16[4,16,1024]{2,1,0:T(8,128)(2,1)} custom-call(bf16[16,16,1152]{2,1,0:T(8,128)(2,1)S(1)} %all-to-all-done.1.got_ref, bf16[1,1024,512]{2,1,0:T(8,128)(2,1)S(1)} %copy-done, bf16[1,512,1024]{2,1,0:T(8,128)(2,1)S(1)} %copy-done.1, bf16[1,1024,512]{2,1,0:T(8,128)(2,1)S(1)} %copy-done.3, bf16[1,512,1024]{2,1,0:T(8,128)(2,1)S(1)} %copy-done.5), custom_call_target="tpu_custom_call" | custom-call | tf_op jit(solution)/shard_map/pallas_call | solution.py:207
  41.2 3.3 %all-to-all-start.2 = ((bf16[4,16,1024]{2,1,0:T(8,128)(2,1)}), bf16[4,16,1024]{2,1,0:T(8,128)(2,1)S(1)}, u32[]{:S(2)}, u32[]{:S(2)}) async-start(bf16[4,16,1024]{2,1,0:T(8,128)(2,1)} %shard_map.47), calls=%async_computation.2 | async-start | bytes 262144 | tf_op jit(solution)/shard_map/all_to_all | solution.py:20
  44.6 0.1 pad_add_fusion.at_ref
  44.6 0.8 shard_map.49
  45.4 2.3 %collective-permute-start.2 = (bf16[272,128]{1,0:T(8,128)(2,1)S(1)}, bf16[272,128]{1,0:T(8,128)(2,1)S(1)}, u32[]{:S(2)}, u32[]{:S(2)}) collective-permute-start(bf16[272,128]{1,0:T(8,128)(2,1)S(1)} %get-tuple-element.25), channel_id=1, source_target_pairs={{0,1},{1,0},{2,3},{3,2},{4,5},{5,4},{6,7},{7,6},{8,9},{9,8},{10,11... | collective-permute-start | bytes 208904 | tf_op jit(solution)/shard_map/ppermute | solution.py:258
  47.8 4.5 %collective-permute-start.3 = (bf16[272,128]{1,0:T(8,128)(2,1)S(1)}, bf16[272,128]{1,0:T(8,128)(2,1)S(1)}, u32[]{:S(2)}, u32[]{:S(2)}) collective-permute-start(bf16[272,128]{1,0:T(8,128)(2,1)S(1)} %get-tuple-element.26), channel_id=1, source_target_pairs={{0,2},{1,3},{2,0},{3,1},{4,6},{5,7},{6,4},{7,5},{8,10},{9,11},{10,... | collective-permute-start | bytes 208904 | tf_op jit(solution)/shard_map/ppermute | solution.py:258
  52.3 2.7 %collective-permute-start.4 = (bf16[272,128]{1,0:T(8,128)(2,1)S(1)}, bf16[272,128]{1,0:T(8,128)(2,1)S(1)}, u32[]{:S(2)}, u32[]{:S(2)}) collective-permute-start(bf16[272,128]{1,0:T(8,128)(2,1)S(1)} %get-tuple-element.27), channel_id=1, source_target_pairs={{0,3},{1,2},{2,1},{3,0},{4,7},{5,6},{6,5},{7,4},{8,11},{9,10},{10,... | collective-permute-start | bytes 208904 | tf_op jit(solution)/shard_map/ppermute | solution.py:258
  55.0 0.0 all-to-all-done.2.got_ref
  55.1 0.1 shard_map.48
  55.2 0.0 collective-permute-done.2.r1
  55.2 0.0 collective-permute-done.3.r2
  55.2 3.4 %collective-permute-done.4.r3 = bf16[272,128]{1,0:T(8,128)(2,1)S(1)} collective-permute-done((bf16[272,128]{1,0:T(8,128)(2,1)S(1)}, bf16[272,128]{1,0:T(8,128)(2,1)S(1)}, u32[]{:S(2)}, u32[]{:S(2)}) %collective-permute-start.4) | collective-permute-done | bytes 69664 | tf_op jit(solution)/shard_map/ppermute | solution.py:258
  58.6 16.1 %all_to_all.21 = bf16[16,32,1024]{2,1,0:T(8,128)(2,1)S(1)} all-to-all(bf16[16,32,1024]{2,1,0:T(8,128)(2,1)S(1)} %shard_map.48), channel_id=1, replica_groups=mesh['x'=4,'zla'=2,'zlb'=2,'c'=2,'zh'=4,'y'=4] {'x','y'}, dimensions={0} | all-to-all | bytes 2097152 | tf_op jit(solution)/shard_map/all_to_all | solution.py:20
  74.7 1.1 shard_map.50
  75.8 8.8 %collective-permute-start.5 = (bf16[2,264,128]{2,1,0:T(8,128)(2,1)S(1)}, bf16[2,264,128]{2,1,0:T(8,128)(2,1)S(1)}, u32[]{:S(2)}, u32[]{:S(2)}) collective-permute-start(bf16[2,264,128]{2,1,0:T(8,128)(2,1)S(1)} %get-tuple-element.34), channel_id=1, source_target_pairs={{0,4},{4,0},{8,12},{12,8},{1,5},{5,1},{9,13},{13,9},{2,6},{6,2},{1... | collective-permute-start | bytes 405512 | tf_op jit(solution)/shard_map/ppermute | solution.py:288
  84.6 7.9 %collective-permute-start.6 = (bf16[2,264,128]{2,1,0:T(8,128)(2,1)S(1)}, bf16[2,264,128]{2,1,0:T(8,128)(2,1)S(1)}, u32[]{:S(2)}, u32[]{:S(2)}) collective-permute-start(bf16[2,264,128]{2,1,0:T(8,128)(2,1)S(1)} %get-tuple-element.35), channel_id=1, source_target_pairs={{0,8},{4,12},{8,0},{12,4},{1,9},{5,13},{9,1},{13,5},{2,10},{6,14},... | collective-permute-start | bytes 405512 | tf_op jit(solution)/shard_map/ppermute | solution.py:288
  92.6 1.9 %collective-permute-start.7 = (bf16[2,264,128]{2,1,0:T(8,128)(2,1)S(1)}, bf16[2,264,128]{2,1,0:T(8,128)(2,1)S(1)}, u32[]{:S(2)}, u32[]{:S(2)}) collective-permute-start(bf16[2,264,128]{2,1,0:T(8,128)(2,1)S(1)} %get-tuple-element.36), channel_id=1, source_target_pairs={{0,12},{4,8},{8,4},{12,0},{1,13},{5,9},{9,5},{13,1},{2,14},{6,10},... | collective-permute-start | bytes 405512 | tf_op jit(solution)/shard_map/ppermute | solution.py:288
  94.5 1.8 %collective-permute-done.5.refs_1_ = bf16[2,264,128]{2,1,0:T(8,128)(2,1)S(1)} collective-permute-done((bf16[2,264,128]{2,1,0:T(8,128)(2,1)S(1)}, bf16[2,264,128]{2,1,0:T(8,128)(2,1)S(1)}, u32[]{:S(2)}, u32[]{:S(2)}) %collective-permute-start.5) | collective-permute-done | bytes 135200 | tf_op jit(solution)/shard_map/ppermute | solution.py:288
  96.3 3.5 %collective-permute-done.6.refs_2_ = bf16[2,264,128]{2,1,0:T(8,128)(2,1)S(1)} collective-permute-done((bf16[2,264,128]{2,1,0:T(8,128)(2,1)S(1)}, bf16[2,264,128]{2,1,0:T(8,128)(2,1)S(1)}, u32[]{:S(2)}, u32[]{:S(2)}) %collective-permute-start.6) | collective-permute-done | bytes 135200 | tf_op jit(solution)/shard_map/ppermute | solution.py:288
  99.8 15.2 %collective-permute-done.7.refs_3_ = bf16[2,264,128]{2,1,0:T(8,128)(2,1)S(1)} collective-permute-done((bf16[2,264,128]{2,1,0:T(8,128)(2,1)S(1)}, bf16[2,264,128]{2,1,0:T(8,128)(2,1)S(1)}, u32[]{:S(2)}, u32[]{:S(2)}) %collective-permute-start.7) | collective-permute-done | bytes 135200 | tf_op jit(solution)/shard_map/ppermute | solution.py:288
  115.0 0.7 shard_map.51
  115.7 4.3 %all-gather = bf16[64,1024]{1,0:T(8,128)(2,1)S(1)} all-gather(bf16[32,1024]{1,0:T(8,128)(2,1)S(1)} %get-tuple-element.38), channel_id=2, replica_groups=mesh['x'=4,'zla'=2,'zlb'=2,'c'=2,'zh'=4,'y'=4] {'c'}, dimensions={0}, use_global_device_ids=true | all-gather | bytes 196608 | tf_op jit(solution)/shard_map/all_gather | solution.py:292
  120.0 1.2 shard_map.52
Async XLA Ops:
  0.0 13.2 %copy-start.6 = (bf16[1024,128]{1,0:T(8,128)(2,1)S(1)}, bf16[1024,128]{1,0:T(8,128)(2,1)}, u32[]{:S(2)}) copy-start(bf16[1024,128]{1,0:T(8,128)(2,1)} %router_ref.1) | copy-start | bytes 786436
  13.2 6.2 %copy-start = (bf16[1,1024,512]{2,1,0:T(8,128)(2,1)S(1)}, bf16[1,1024,512]{2,1,0:T(8,128)(2,1)}, u32[]{:S(2)}) copy-start(bf16[1,1024,512]{2,1,0:T(8,128)(2,1)} %a_ref.1) | copy-start | bytes 3145732
  13.2 8.5 %copy-start.1 = (bf16[1,512,1024]{2,1,0:T(8,128)(2,1)S(1)}, bf16[1,512,1024]{2,1,0:T(8,128)(2,1)}, u32[]{:S(2)}) copy-start(bf16[1,512,1024]{2,1,0:T(8,128)(2,1)} %b_ref.1) | copy-start | bytes 3145732
  15.8 20.9 %all-to-all-start.1 = ((bf16[16,16,1152]{2,1,0:T(8,128)(2,1)}), bf16[16,16,1152]{2,1,0:T(8,128)(2,1)S(1)}, u32[]{:S(2)}, u32[]{:S(2)}) async-start(bf16[16,16,1152]{2,1,0:T(8,128)(2,1)} %get-tuple-element.22), calls=%async_computation.1 | async-start | bytes 1179648 | tf_op jit(solution)/shard_map/all_to_all | solution.py:20
  19.4 4.6 %collective-permute-start = (bf16[1,1024,512]{2,1,0:T(8,128)(2,1)S(1)}, bf16[1,1024,512]{2,1,0:T(8,128)(2,1)S(1)}, u32[]{:S(2)}, u32[]{:S(2)}) collective-permute-start(bf16[1,1024,512]{2,1,0:T(8,128)(2,1)S(1)} %copy-done), channel_id=1, source_target_pairs={{0,16},{16,0},{1,17},{17,1},{2,18},{18,2},{3,19},{19,3},{4,20},{20... | collective-permute-start | bytes 3145736 | tf_op jit(solution)/shard_map/ppermute | solution.py:243
  21.7 4.6 %collective-permute-start.1 = (bf16[1,512,1024]{2,1,0:T(8,128)(2,1)S(1)}, bf16[1,512,1024]{2,1,0:T(8,128)(2,1)S(1)}, u32[]{:S(2)}, u32[]{:S(2)}) collective-permute-start(bf16[1,512,1024]{2,1,0:T(8,128)(2,1)S(1)} %copy-done.1), channel_id=1, source_target_pairs={{0,16},{16,0},{1,17},{17,1},{2,18},{18,2},{3,19},{19,3},{4,20},{20... | collective-permute-start | bytes 3145736 | tf_op jit(solution)/shard_map/ppermute | solution.py:244
  24.0 1.0 copy-start.2
  26.3 1.0 copy-start.4
  36.7 1.2 %copy-start.3 = (bf16[1,1024,512]{2,1,0:T(8,128)(2,1)S(1)}, bf16[1,1024,512]{2,1,0:T(8,128)(2,1)}, u32[]{:S(2)}) copy-start(bf16[1,1024,512]{2,1,0:T(8,128)(2,1)} %copy-done.2) | copy-start | bytes 3145732
  37.9 1.2 %copy-start.5 = (bf16[1,512,1024]{2,1,0:T(8,128)(2,1)S(1)}, bf16[1,512,1024]{2,1,0:T(8,128)(2,1)}, u32[]{:S(2)}) copy-start(bf16[1,512,1024]{2,1,0:T(8,128)(2,1)} %copy-done.4) | copy-start | bytes 3145732
  41.2 13.8 %all-to-all-start.2 = ((bf16[4,16,1024]{2,1,0:T(8,128)(2,1)}), bf16[4,16,1024]{2,1,0:T(8,128)(2,1)S(1)}, u32[]{:S(2)}, u32[]{:S(2)}) async-start(bf16[4,16,1024]{2,1,0:T(8,128)(2,1)} %shard_map.47), calls=%async_computation.2 | async-start | bytes 262144 | tf_op jit(solution)/shard_map/all_to_all | solution.py:20
  45.4 9.7 %collective-permute-start.2 = (bf16[272,128]{1,0:T(8,128)(2,1)S(1)}, bf16[272,128]{1,0:T(8,128)(2,1)S(1)}, u32[]{:S(2)}, u32[]{:S(2)}) collective-permute-start(bf16[272,128]{1,0:T(8,128)(2,1)S(1)} %get-tuple-element.25), channel_id=1, source_target_pairs={{0,1},{1,0},{2,3},{3,2},{4,5},{5,4},{6,7},{7,6},{8,9},{9,8},{10,11... | collective-permute-start | bytes 208904 | tf_op jit(solution)/shard_map/ppermute | solution.py:258
  47.8 7.4 %collective-permute-start.3 = (bf16[272,128]{1,0:T(8,128)(2,1)S(1)}, bf16[272,128]{1,0:T(8,128)(2,1)S(1)}, u32[]{:S(2)}, u32[]{:S(2)}) collective-permute-start(bf16[272,128]{1,0:T(8,128)(2,1)S(1)} %get-tuple-element.26), channel_id=1, source_target_pairs={{0,2},{1,3},{2,0},{3,1},{4,6},{5,7},{6,4},{7,5},{8,10},{9,11},{10,... | collective-permute-start | bytes 208904 | tf_op jit(solution)/shard_map/ppermute | solution.py:258
  52.3 6.3 %collective-permute-start.4 = (bf16[272,128]{1,0:T(8,128)(2,1)S(1)}, bf16[272,128]{1,0:T(8,128)(2,1)S(1)}, u32[]{:S(2)}, u32[]{:S(2)}) collective-permute-start(bf16[272,128]{1,0:T(8,128)(2,1)S(1)} %get-tuple-element.27), channel_id=1, source_target_pairs={{0,3},{1,2},{2,1},{3,0},{4,7},{5,6},{6,5},{7,4},{8,11},{9,10},{10,... | collective-permute-start | bytes 208904 | tf_op jit(solution)/shard_map/ppermute | solution.py:258
  75.8 20.5 %collective-permute-start.5 = (bf16[2,264,128]{2,1,0:T(8,128)(2,1)S(1)}, bf16[2,264,128]{2,1,0:T(8,128)(2,1)S(1)}, u32[]{:S(2)}, u32[]{:S(2)}) collective-permute-start(bf16[2,264,128]{2,1,0:T(8,128)(2,1)S(1)} %get-tuple-element.34), channel_id=1, source_target_pairs={{0,4},{4,0},{8,12},{12,8},{1,5},{5,1},{9,13},{13,9},{2,6},{6,2},{1... | collective-permute-start | bytes 405512 | tf_op jit(solution)/shard_map/ppermute | solution.py:288
  84.6 15.2 %collective-permute-start.6 = (bf16[2,264,128]{2,1,0:T(8,128)(2,1)S(1)}, bf16[2,264,128]{2,1,0:T(8,128)(2,1)S(1)}, u32[]{:S(2)}, u32[]{:S(2)}) collective-permute-start(bf16[2,264,128]{2,1,0:T(8,128)(2,1)S(1)} %get-tuple-element.35), channel_id=1, source_target_pairs={{0,8},{4,12},{8,0},{12,4},{1,9},{5,13},{9,1},{13,5},{2,10},{6,14},... | collective-permute-start | bytes 405512 | tf_op jit(solution)/shard_map/ppermute | solution.py:288
  92.6 22.4 %collective-permute-start.7 = (bf16[2,264,128]{2,1,0:T(8,128)(2,1)S(1)}, bf16[2,264,128]{2,1,0:T(8,128)(2,1)S(1)}, u32[]{:S(2)}, u32[]{:S(2)}) collective-permute-start(bf16[2,264,128]{2,1,0:T(8,128)(2,1)S(1)} %get-tuple-element.36), channel_id=1, source_target_pairs={{0,12},{4,8},{8,4},{12,0},{1,13},{5,9},{9,5},{13,1},{2,14},{6,10},... | collective-permute-start | bytes 405512 | tf_op jit(solution)/shard_map/ppermute | solution.py:288
